TPU v7x, 256 devices: a whole 4x4x8 slice. The times are simulated.
256 devices in a mesh: expert: 64 (over z, y, core), tensor: 4 (over x).
Axes of the slice: x: 4, y: 4, z: 8, core: 2. Of those that a mesh axis runs over, the one named last changes fastest.
Arguments:
- tokens: bfloat16 [8192, 2048], P('expert', 'tensor'), may hold values from -6 to 6
- grad_out: bfloat16 [8192, 2048], P('expert', 'tensor'), may hold values from -1.1953125 to 1.1953125
- routes: int32 [8192, 2], P('expert'), may hold values from 0 to 15, all different within a row; in each aligned block of 128 rows (0 to 127, 128 to 255, ...) at most 20 rows name the same one
- gates: float32 [8192, 2], P('expert'), may hold values from 0.1 to 1
- w_up: bfloat16 [2048, 131072], P(None, ('expert', 'tensor')), may hold values from -0.125 to 0.125
- w_down: bfloat16 [131072, 2048], P(('expert', 'tensor')), may hold values from -0.0625 to 0.0625
Outputs:
- grad_tokens: bfloat16 [8192, 2048], P('expert', 'tensor')
- grad_up: float32 [2048, 131072], P(None, ('expert', 'tensor'))
- grad_down: float32 [131072, 2048], P(('expert', 'tensor'))
Inputs may be any that keep to these rules, and one draw needn't show every extreme that they name: `routes`: the two experts of a token differ. Among the tokens of one index of the expert axis no expert is named more than 20 times, and in every draw some expert is named exactly 20 times by the tokens of some index.
All inputs are finite; a program needn't handle non-finite values.
Results may differ from a plain program's by a relative error of at most 0.012.
Values may be sent and summed in bfloat16 or wider, within the bound.
A program may use at most 128 MiB of HBM per device.

v0:
```python
import jax
import jax.numpy as jnp
from jax import lax
from jax.sharding import PartitionSpec as P

EXP_FULL = 16


root_half = 0.7071067811865476
gauss_norm = 0.3989422804014327


def split_up(x, dim, size):
    shape = x.shape
    tiles = x.reshape(*shape[:dim], size, shape[dim] // size, *shape[dim + 1 :])
    return jnp.moveaxis(tiles, dim, 0)


def sum_at_owner(x, axis, dim):
    size = lax.axis_size(axis)
    tiles = lax.all_to_all(split_up(x, dim, size), axis, 0, 0, tiled=True)
    return jnp.sum(tiles.astype(jnp.float32), axis=0)


def gelu_value(v):
    return 0.5 * v * (1.0 + lax.erf(v * root_half))


def gelu_slope(v):
    return 0.5 * (1.0 + lax.erf(v * root_half)) + v * jnp.exp(-0.5 * v * v) * gauss_norm


def local(tokens, grad_out, routes, gates, w_up, w_down):
    expert_count = lax.axis_size("expert")
    experts = min(EXP_FULL, expert_count)
    group = expert_count // experts
    tok_dev = routes.shape[0]
    choose = routes.shape[1]
    capacity = group * (5 * tok_dev // (2 * expert_count))
    flat = routes.reshape(-1)
    onehot = (flat[:, None] == jnp.arange(experts, dtype=jnp.int32)[None, :]).astype(jnp.int32)
    rank = jnp.cumsum(onehot, axis=0, dtype=jnp.int32) - onehot
    dest = flat * capacity + jnp.sum(rank * onehot, axis=1)
    select = (jnp.arange(experts * capacity, dtype=jnp.int32)[:, None] == dest[None, :]).astype(
        jnp.bfloat16
    )
    full_tok, full_grad = (tokens, grad_out)
    width = full_tok.shape[1]
    repeated = jnp.repeat(full_tok, choose, axis=0)
    scaled = (full_grad[:, None, :].astype(jnp.float32) * gates[:, :, None]).astype(jnp.bfloat16)
    scaled = scaled.reshape(tok_dev * choose, width)
    packed = (
        jnp.stack(
            [
                jnp.dot(select, repeated, preferred_element_type=jnp.float32),
                jnp.dot(select, scaled, preferred_element_type=jnp.float32),
            ]
        )
        .astype(jnp.bfloat16)
        .reshape(2, experts, capacity, width)
    )
    outgoing = jnp.repeat(packed, group, axis=1)
    arrived = lax.all_to_all(outgoing, "expert", split_axis=1, concat_axis=1, tiled=True)
    arrived = lax.all_gather(arrived, "tensor", axis=3, tiled=True)
    rows = arrived.reshape(2, expert_count * capacity, arrived.shape[3])
    rows_x = rows[0]
    rows_y = rows[1]
    pre = jnp.dot(rows_x, w_up, preferred_element_type=jnp.float32)
    act = gelu_value(pre).astype(jnp.bfloat16)
    d_act = lax.dot_general(
        rows_y, w_down, (((1,), (1,)), ((), ())), preferred_element_type=jnp.float32
    )
    d_pre = (d_act * gelu_slope(pre)).astype(jnp.bfloat16)
    grad_up = lax.dot_general(
        rows_x, d_pre, (((0,), (0,)), ((), ())), preferred_element_type=jnp.float32
    )
    grad_down = lax.dot_general(
        act, rows_y, (((0,), (0,)), ((), ())), preferred_element_type=jnp.float32
    )
    partial_value = lax.dot_general(
        d_pre, w_up, (((1,), (1,)), ((), ())), preferred_element_type=jnp.float32
    )
    partial_value = lax.optimization_barrier(partial_value.astype(jnp.bfloat16)).astype(jnp.float32)
    summed = sum_at_owner(partial_value.astype(jnp.bfloat16), "tensor", 1)
    quarter = summed.shape[1]
    back = summed.reshape(expert_count, capacity, quarter)
    returned = lax.all_to_all(
        back.astype(jnp.bfloat16), "expert", split_axis=0, concat_axis=0, tiled=True
    ).astype(back.dtype)
    combined = returned.reshape(experts, group, capacity, quarter).sum(axis=1)
    combined = combined.reshape(experts * capacity, quarter)
    grad_tokens = combined[dest].reshape(tok_dev, choose, quarter).sum(axis=1).astype(jnp.bfloat16)
    return (grad_tokens, grad_up, grad_down)


def solution(mesh):
    return jax.shard_map(
        local,
        mesh=mesh,
        in_specs=(
            P("expert", "tensor"),
            P("expert", "tensor"),
            P("expert", None),
            P("expert", None),
            P(None, ("expert", "tensor")),
            P(("expert", "tensor"), None),
        ),
        out_specs=(
            P("expert", "tensor"),
            P(None, ("expert", "tensor")),
            P(("expert", "tensor"), None),
        ),
        check_vma=False,
    )
```

profile of v0, /device:TPU:1, one launch (start us, length us, event | category | flops | bytes accessed | tf_op | source)
XLA Modules:
  0.0 406.1 jit_solution(18192644028344596392)
XLA Ops:
  7.2 0.9 copy.14
  8.3 0.1 reshape.145
  8.5 0.6 reduce-window.6
  9.0 0.2 slice_reduce_fusion.2
  9.4 1.0 mul.84
  10.4 0.4 mul.85
  10.8 0.8 copy.17
  11.7 1.0 broadcast_in_dim.4
  12.9 0.3 fusion.7
  13.2 0.3 fusion.8
  13.6 0.7 copy.18
  14.3 1.6 broadcast_in_dim.5
  15.9 75.8 %all_to_all.15 = bf16[2,64,20,512]{3,0,2,1:T(2,128)(2,1)} all-to-all(bf16[2,64,20,512]{3,0,2,1:T(2,128)(2,1)S(1)} %bitcast.52), channel_id=1, replica_groups=mesh['expert'=64,'tensor'=4] {'expert'}, dimensions={1} | all-to-all | bytes 5242880 | tf_op jit(solution)/shard_map/all_to_all | solution.py:63
  91.7 101.8 %all-gather.2.cloned.1.call-done = bf16[2,64,20,2048]{3,0,2,1:T(2,128)(2,1)} async-done(((bf16[2,64,20,512]{3,0,2,1:T(2,128)(2,1)}), bf16[2,64,20,2048]{3,0,2,1:T(2,128)(2,1)}) %all-gather.2.cloned.1.call-update) | async-done | bytes 10485776 | tf_op jit(solution)/shard_map/all_gather | solution.py:64
  193.5 52.4 %slice_reduce_fusion = (bf16[64,20,2048]{2,1,0:T(8,128)(2,1)}, bf16[64,20,2048]{2,1,0:T(8,128)(2,1)}) fusion(bf16[2,64,20,2048]{3,0,2,1:T(2,128)(2,1)} %all-gather.2.cloned.1.call-done), kind=kLoop, calls=%fused_computation.1 | loop fusion | bytes 20971520 | tf_op jit(solution)/shard_map/slice | solution.py:66
  245.9 9.0 %squeeze.7 = bf16[1280,2048]{1,0:T(8,128)(2,1)} reshape(bf16[64,20,2048]{2,1,0:T(8,128)(2,1)} %get-tuple-element.3) | data formatting | bytes 10485760 | tf_op jit(solution)/shard_map/squeeze | solution.py:66
  254.9 9.0 %squeeze.6 = bf16[1280,2048]{1,0:T(8,128)(2,1)} reshape(bf16[64,20,2048]{2,1,0:T(8,128)(2,1)} %get-tuple-element.4) | data formatting | bytes 10485760 | tf_op jit(solution)/shard_map/squeeze | solution.py:67
  263.9 4.9 %fusion.23 = f32[1280,512]{1,0:T(8,128)S(1)} fusion(bf16[1280,2048]{1,0:T(8,128)(2,1)} %squeeze.7, bf16[2048,512]{1,0:T(8,128)(2,1)S(1)} %copy-done), kind=kOutput, calls=%fused_computation.46 | convolution fusion | flops 2684354560 | bytes 9961472 | tf_op jit(solution)/shard_map/dot_general | solution.py:68
  268.9 3.9 fusion
  272.8 3.2 convolution_convert_fusion
  276.0 0.5 copy.27
  276.5 61.2 %all_to_all.16 = bf16[4,1280,512]{2,1,0:T(8,128)(2,1)} all-to-all(bf16[4,1280,512]{2,1,0:T(8,128)(2,1)S(1)} %bitcast.51), channel_id=1, replica_groups=mesh['expert'=64,'tensor'=4] {'tensor'}, dimensions={0} | all-to-all | bytes 10485760 | tf_op jit(solution)/shard_map/all_to_all | solution.py:21
  337.7 4.2 %reduce_sum.42 = bf16[1280,512]{1,0:T(8,128)(2,1)S(1)} reduce(bf16[4,1280,512]{2,1,0:T(8,128)(2,1)} %all_to_all.16, bf16[]{:T(256)} %constant.24.clone.1), dimensions={0}, to_apply=%region_3.4 | reduce | flops 1966080 | bytes 6553602 | tf_op jit(solution)/shard_map/reduce_sum | solution.py:22
  341.9 1.3 convert_element_type.46
  343.2 14.1 %all-to-all-start.2 = ((bf16[64,20,512]{2,1,0:T(8,128)(2,1)}), bf16[64,20,512]{2,1,0:T(8,128)(2,1)S(1)}, u32[]{:S(2)}, u32[]{:S(2)}) async-start(bf16[64,20,512]{2,1,0:T(8,128)(2,1)} %convert_element_type.46), calls=%async_computation.2 | async-start | bytes 3145728 | tf_op jit(solution)/shard_map/all_to_all | solution.py:87
  357.6 8.0 %fusion.24 = f32[2048,512]{1,0:T(8,128)} fusion(bf16[1280,2048]{1,0:T(8,128)(2,1)} %squeeze.7, bf16[1280,512]{1,0:T(8,128)(2,1)} %copy-done.7), kind=kOutput, calls=%fused_computation.47 | convolution fusion | flops 2684354560 | bytes 10747904 | tf_op jit(solution)/shard_map/dot_general | solution.py:74
  365.6 4.5 %fusion.5 = f32[512,2048]{1,0:T(8,128)} fusion(bf16[1280,2048]{1,0:T(8,128)(2,1)S(1)} %bitcast.50, f32[1280,512]{1,0:T(8,128)S(1)} %copy-done.4), kind=kOutput, calls=%fused_computation.15 | convolution fusion | flops 2687631360 | bytes 12058624 | tf_op jit(solution)/shard_map/dot_general | solution.py:77
  370.1 26.2 %all-to-all-done.2 = bf16[64,20,512]{2,1,0:T(8,128)(2,1)S(1)} async-done(((bf16[64,20,512]{2,1,0:T(8,128)(2,1)}), bf16[64,20,512]{2,1,0:T(8,128)(2,1)S(1)}, u32[]{:S(2)}, u32[]{:S(2)}) %all-to-all-start.2) | async-done | bytes 1310752 | tf_op jit(solution)/shard_map/all_to_all | solution.py:87
  396.3 0.3 convert_reduce_fusion
  396.7 1.0 gather_fusion
  397.6 0.3 reshape.153
  397.9 1.3 reduce_sum.45
  (39 shorter events, 1.1 us)
Async XLA Ops:
  7.2 256.7 %copy-start = (bf16[2048,512]{1,0:T(8,128)(2,1)S(1)}, bf16[2048,512]{1,0:T(8,128)(2,1)}, u32[]{:S(2)}) copy-start(bf16[2048,512]{1,0:T(8,128)(2,1)} %param.10) | copy-start | bytes 6291460
  7.2 186.3 %all-gather.2.cloned.1.call-start = ((), (), s32[]{:S(2)}) async-start(), calls=%async_computation.3 | async-start | bytes 13107200 | tf_op jit(solution)/shard_map/all_gather | solution.py:64
  263.9 5.0 %copy-start.2 = (bf16[1280,2048]{1,0:T(8,128)(2,1)S(1)}, bf16[1280,2048]{1,0:T(8,128)(2,1)}, u32[]{:S(2)}) copy-start(bf16[1280,2048]{1,0:T(8,128)(2,1)} %squeeze.6) | copy-start | bytes 15728644
  263.9 5.0 %copy-start.6 = (bf16[512,2048]{1,0:T(8,128)(2,1)S(1)}, bf16[512,2048]{1,0:T(8,128)(2,1)}, u32[]{:S(2)}) copy-start(bf16[512,2048]{1,0:T(8,128)(2,1)} %param.11) | copy-start | bytes 6291460
  268.9 3.9 copy-start.3
  272.7 3.2 copy-start.7
  341.8 15.4 %copy-start.5 = (s32[128,2]{0,1:T(2,128)S(1)}, s32[128,2]{0,1:T(2,128)}, u32[]{:S(2)}) copy-start(s32[128,2]{0,1:T(2,128)} %param.8) | copy-start | bytes 3076
  343.2 22.4 %slice-start = ((s8[5242880]{0:T(1024)(128)(4,1)}), s8[1048576]{0:T(1024)(128)(4,1)S(1)}, s32[]{:S(2)}) async-start(s8[5242880]{0:T(1024)(128)(4,1)} %bitcast.49), calls=%async_computation.4 | async-start | bytes 2097152
  343.2 53.2 %all-to-all-start.2 = ((bf16[64,20,512]{2,1,0:T(8,128)(2,1)}), bf16[64,20,512]{2,1,0:T(8,128)(2,1)S(1)}, u32[]{:S(2)}, u32[]{:S(2)}) async-start(bf16[64,20,512]{2,1,0:T(8,128)(2,1)} %convert_element_type.46), calls=%async_computation.2 | async-start | bytes 3145728 | tf_op jit(solution)/shard_map/all_to_all | solution.py:87
  357.6 8.0 %slice-start.1 = ((s8[5242880]{0:T(1024)(128)(4,1)}), s8[4194304]{0:T(1024)(128)(4,1)S(1)}, s32[]{:S(2)}) async-start(s8[5242880]{0:T(1024)(128)(4,1)} %bitcast.49), calls=%async_computation.5 | async-start | bytes 8388608
  357.6 8.0 %copy-start.4 = (f32[1280,512]{1,0:T(8,128)S(1)}, f32[1280,512]{1,0:T(8,128)}, u32[]{:S(2)}) copy-start(f32[1280,512]{1,0:T(8,128)} %copy-done.3) | copy-start | bytes 7864324
  396.6 2.7 copy-start.1
Sparse Core Ops, SparseCore 0:
  91.9 101.5 all-gather.1
where the time goes:
time: 407 us; the launch traced here: 406 us
  blocking collectives  137 us (34%)
  waiting for transfers between devices  128 us (31%)
  local copies, waits for them, and re-layouts  81 us (20%)
  matrix products  25.2 us (6%)
  between operations  14.3 us (4%)
  starting transfers between devices  14.1 us (3%)
  other arithmetic  6.57 us (2%)
    all_gather x1, waiting for transfers between devices, local(): arrived = lax.all_gather(arrived, 'tensor', axis=3, tiled=True)  102 us
    all_to_all x1, blocking collectives, local(): lax.all_to_all(outgoing, 'expert', split_axis=1, concat_axis=1, tiled=True)  75.8 us
    all_to_all x1, blocking collectives, sum_at_owner(): tiles = lax.all_to_all(split_up(x, dim, size), axis, 0, 0, tiled=True)  61.2 us
    slice x1, local copies, waits for them, and re-layouts, local(): rows_x = rows[0]  52.4 us
    all_to_all x1, waiting for transfers between devices, local(): lax.all_to_all(back.astype(jnp.bfloat16), 'expert', split_axis=0, concat_...  26.2 us
    all_to_all x1, starting transfers between devices, local(): lax.all_to_all(back.astype(jnp.bfloat16), 'expert', split_axis=0, concat_...  14.1 us
    squeeze x1, local copies, waits for them, and re-layouts, local(): rows_y = rows[1]  9 us
    squeeze x1, local copies, waits for them, and re-layouts, local(): rows_x = rows[0]  8.99 us
  transfers between devices with their start and end apart: 2, of which 2 were waited for; matrix products, arithmetic and copies ran while one was open for 3% of the time, Pallas kernels for 0%

commit v1 on v0

v1 whole, which is shorter than its diff:
```python
import jax
import jax.numpy as jnp
from jax import lax
from jax.experimental import pallas as pl
from jax.experimental.pallas import tpu as pltpu
from jax.sharding import PartitionSpec as P

MESH = pl.DeviceIdType.MESH
Z, Y, X = 8, 4, 4
CAP, PAIR = 20, 40
EXPERTS = 16
BLOCKS = 32
TOK = 128
QUARTER = 512
HALF = 256
D = 2048
NEAR = (0, 1, 7, 2, 6, 3, 5, 4)

root_half = 0.7071067811865476
gauss_norm = 0.3989422804014327


def gelu_value(v):
    return 0.5 * v * (1.0 + lax.erf(v * root_half))


def gelu_slope(v):
    return 0.5 * (1.0 + lax.erf(v * root_half)) + v * jnp.exp(-0.5 * v * v) * gauss_norm


def place():
    e = lax.axis_index("expert")
    x = lax.axis_index("tensor")
    return e // 8, (e // 2) % 4, e % 2, x


def device(z, y, c, x):
    return ((z * Y + y) * 2 + c, x)


class Net:
    def __init__(self, send_sem, recv_sem):
        self.send_sem, self.recv_sem, self.count, self.sent = send_sem, recv_sem, 0, []

    def number(self):
        self.count += 1
        return self.count - 1

    def send(self, src, dst, target, start=True):
        i = self.number()
        copy = pltpu.make_async_remote_copy(
            src_ref=src,
            dst_ref=dst,
            send_sem=self.send_sem.at[i],
            recv_sem=self.recv_sem.at[i],
            device_id=target,
            device_id_type=MESH,
        )
        if start:
            copy.start()
        self.sent.append(copy)
        return copy

    def finish(self):
        for copy in self.sent:
            copy.wait_send()


def meet(z, y, c, x):
    barrier = pltpu.get_barrier_semaphore()
    partner = y + 1 - 2 * (y % 2)
    others = [
        device(z, y, 1 - c, x),
        device(z, partner, c, x),
        device(z, y, c, (x + 1) % X),
        device(z, y, c, (x + 3) % X),
    ]
    for dz in range(Z):
        for j in range(2):
            if dz or j:
                others.append(device((z + dz) % Z, y if j == 0 else 3 - y, c, x))
    for other in others:
        pl.semaphore_signal(barrier, inc=1, device_id=other, device_id_type=MESH)
    pl.semaphore_wait(barrier, len(others))


def gather_kernel(
    routes, gates, tok, grad, xy, sel, route_buf, gate_buf, values, slots, send_sem, recv_sem, own_sem
):
    z, y, c, x = place()
    k = ((y + 1) // 2) % 2
    partner = y + 1 - 2 * (y % 2)
    net = Net(send_sem, recv_sem)
    meet(z, y, c, x)

    mate = device(z, y, 1 - c, x)
    first = net.send(routes, route_buf.at[c], mate)
    second = net.send(gates, gate_buf.at[c], mate)
    i = net.number()

    def value_copy(src):
        return pltpu.make_async_remote_copy(
            src_ref=src,
            dst_ref=values.at[c],
            send_sem=send_sem.at[i],
            recv_sem=recv_sem.at[i],
            device_id=mate,
            device_id_type=MESH,
        )

    @pl.when(c == 0)
    def _():
        value_copy(grad).start()

    @pl.when(c == 1)
    def _():
        value_copy(tok).start()

    third = value_copy(tok)
    net.sent.append(third)
    route_buf[c] = routes[...]
    gate_buf[c] = gates[...]
    values[c] = jnp.where(c == 0, tok[...], grad[...])
    first.wait_recv()
    second.wait_recv()
    third.wait_recv()

    row = lax.broadcasted_iota(jnp.int32, (EXPERTS * PAIR, TOK), 0)
    expert = lax.broadcasted_iota(jnp.int32, (EXPERTS, TOK), 0)
    before = (
        lax.broadcasted_iota(jnp.int32, (TOK, TOK), 0)
        < lax.broadcasted_iota(jnp.int32, (TOK, TOK), 1)
    ).astype(jnp.bfloat16)
    scale = jnp.zeros((EXPERTS * PAIR, 1), jnp.float32)
    total = jnp.zeros((EXPERTS * PAIR, QUARTER), jnp.float32)
    for s in range(2):
        r = route_buf[s]
        g = gate_buf[s]
        named0 = (expert == r[0:1]).astype(jnp.float32)
        named1 = (expert == r[1:2]).astype(jnp.float32)
        earlier = jnp.dot(
            (named0 + named1).astype(jnp.bfloat16), before, preferred_element_type=jnp.float32
        )
        slot0 = jnp.sum(named0 * earlier, axis=0, keepdims=True).astype(jnp.int32)
        slot1 = jnp.sum(named1 * earlier, axis=0, keepdims=True).astype(jnp.int32)
        hit0 = row == r[0:1] * PAIR + s * CAP + slot0
        hit1 = row == r[1:2] * PAIR + s * CAP + slot1
        pick = jnp.where(hit0 | hit1, 1.0, 0.0).astype(jnp.bfloat16)
        weight = jnp.where(hit0, g[0:1], 0.0) + jnp.where(hit1, g[1:2], 0.0)
        scale = scale + jnp.sum(weight, axis=1, keepdims=True)
        sel[:, s * TOK : (s + 1) * TOK] = pick
        total = total + jnp.dot(pick, values[s], preferred_element_type=jnp.float32)
    total = total * jnp.where(c == 0, 1.0, scale)
    slots[...] = total.astype(jnp.bfloat16).reshape(EXPERTS, PAIR, QUARTER)

    def cols(q):
        return pl.ds(pl.multiple_of(q * QUARTER, QUARTER), QUARTER)

    arrivals = {}
    mine = z * 4 + k * 2 + y // 2
    own_copy = None
    for dz in NEAR:
        ze = (z + dz) % Z
        for j in range(2):
            expert_id = ze * 2 + (y // 2 if j == 0 else 1 - y // 2)
            src = slots.at[expert_id]
            dst = xy.at[c, mine, :, cols(x)]
            if dz == 0 and j == 0:
                own_copy = pltpu.make_async_copy(src, dst, own_sem)
                own_copy.start()
            else:
                arrivals[dz, j] = net.send(src, dst, device(ze, y if j == 0 else 3 - y, c, x))

    right, left = (x + 1) % X, (x + 3) % X
    far = (x + 2) % X
    to_right, to_left = device(z, y, c, right), device(z, y, c, left)
    to_y = device(z, partner, c, x)
    live = [dict() for _ in NEAR]

    def part(block, count, q):
        return xy.at[c, pl.ds(block, count), :, cols(q)]

    def both(block, count, q, target):
        return net.send(part(block, count, q), part(block, count, q), target)

    def step_a(n):
        dz, at = NEAR[n], live[n]
        if dz == 0:
            own_copy.wait()
        else:
            arrivals[dz, 0].wait_recv()
        arrivals[dz, 1].wait_recv()
        base = ((z + Z - dz) % Z) * 4
        at["base"], at["own"], at["other"] = base, base + k * 2, base + (1 - k) * 2
        at["r"] = both(at["own"], 2, x, to_right)
        at["l"] = both(at["own"], 2, x, to_left)
        at["y"] = both(at["own"], 2, x, to_y)

    def step_b(n):
        at = live[n]
        at["r"].wait_recv()
        at["l"].wait_recv()
        if n % 2 == 0:
            at["y"].wait_recv()
            at["r2"] = both(at["other"], 2, x, to_right)
            at["l2"] = both(at["other"], 2, x, to_left)
        else:
            at["fr"] = both(at["own"], 1, left, to_right)
            at["fl"] = both(at["own"] + 1, 1, right, to_left)
            at["y1"] = both(at["own"], 2, left, to_y)
            at["y2"] = both(at["own"], 2, right, to_y)

    def step_c(n):
        at = live[n]
        if n % 2 == 0:
            at["r2"].wait_recv()
            at["l2"].wait_recv()
            at["fr"] = both(at["base"], 2, left, to_right)
            at["fl"] = both(at["base"] + 2, 2, right, to_left)
        else:
            at["fr"].wait_recv()
            at["fl"].wait_recv()
            at["y3"] = both(at["own"], 2, far, to_y)

    def step_d(n):
        at = live[n]
        if n % 2 == 0:
            at["fr"].wait_recv()
            at["fl"].wait_recv()
        else:
            for name in ("y", "y1", "y2", "y3"):
                at[name].wait_recv()
        rows = xy.at[c, pl.ds(at["base"], 4)]
        at["mate"] = net.send(rows, rows, mate)

    for i in range(len(NEAR) + 3):
        for lag, step in ((3, step_d), (2, step_c), (1, step_b), (0, step_a)):
            if 0 <= i - lag < len(NEAR):
                step(i - lag)
    for at in live:
        at["mate"].wait_recv()
    net.finish()


def return_kernel(
    partial, sel, out, acc, from_mate, hop_a, hop_b, from_y, slots, result, final, send_sem, recv_sem, own_sem
):
    z, y, c, x = place()
    k = ((y + 1) // 2) % 2
    partner = y + 1 - 2 * (y % 2)
    net = Net(send_sem, recv_sem)
    meet(z, y, c, x)
    mate = device(z, y, 1 - c, x)
    right, left = (x + 1) % X, (x + 3) % X
    far = (x + 2) % X
    to_right, to_left = device(z, y, c, right), device(z, y, c, left)
    to_y = device(z, partner, c, x)
    order = NEAR[::-1]
    live = [dict() for _ in order]

    def cols(q, core):
        return pl.ds(pl.multiple_of(q * QUARTER + core * HALF, HALF), HALF)

    def add(ref, other):
        ref[...] = (ref[...].astype(jnp.float32) + other[...].astype(jnp.float32)).astype(jnp.bfloat16)

    for n, dz in enumerate(order):
        base = ((z + dz) % Z) * 4
        live[n]["base"] = base
        live[n]["mate"] = [
            net.send(
                partial.at[pl.ds(base, 4), :, cols(q, 1 - c)], from_mate.at[q, pl.ds(base, 4)], mate
            )
            for q in range(4)
        ]

    def step_a(n):
        at = live[n]
        base = at["base"]
        for q in range(4):
            at["mate"][q].wait_recv()
            acc[q, pl.ds(base, 4)] = (
                partial[pl.ds(base, 4), :, cols(q, c)].astype(jnp.float32)
                + from_mate[q, pl.ds(base, 4)].astype(jnp.float32)
            ).astype(jnp.bfloat16)
        at["ar"] = net.send(acc.at[far, pl.ds(base, 2)], hop_a.at[n, 0], to_right)
        at["al"] = net.send(acc.at[far, pl.ds(base + 2, 2)], hop_a.at[n, 1], to_left)

    def step_b(n):
        at = live[n]
        base = at["base"]
        at["ar"].wait_recv()
        add(acc.at[right, pl.ds(base, 2)], hop_a.at[n, 0])
        at["al"].wait_recv()
        add(acc.at[left, pl.ds(base + 2, 2)], hop_a.at[n, 1])
        at["br"] = net.send(acc.at[right, pl.ds(base, 4)], hop_b.at[n, 0], to_right)
        at["bl"] = net.send(acc.at[left, pl.ds(base, 4)], hop_b.at[n, 1], to_left)

    def step_c(n):
        at = live[n]
        base = at["base"]
        at["br"].wait_recv()
        at["bl"].wait_recv()
        ref = acc.at[x, pl.ds(base, 4)]
        ref[...] = (
            ref[...].astype(jnp.float32)
            + hop_b[n, 0].astype(jnp.float32)
            + hop_b[n, 1].astype(jnp.float32)
        ).astype(jnp.bfloat16)
        at["y"] = net.send(acc.at[x, pl.ds(base + (1 - k) * 2, 2)], from_y.at[n], to_y)

    me = z * 2 + y // 2

    def step_d(n):
        at, dz = live[n], order[n]
        base = at["base"] + k * 2
        at["y"].wait_recv()
        add(acc.at[x, pl.ds(base, 2)], from_y.at[n])
        zs = (z + dz) % Z
        at["back"] = []
        for j in range(2):
            src = acc.at[x, base + (y // 2 if j == 0 else 1 - y // 2)]
            dst = slots.at[me]
            if dz == 0 and j == 0:
                copy = pltpu.make_async_copy(src, dst, own_sem)
                copy.start()
                at["local"] = copy
            else:
                at["back"].append(net.send(src, dst, device(zs, y if j == 0 else 3 - y, c, x)))

    for i in range(len(order) + 3):
        for lag, step in ((3, step_d), (2, step_c), (1, step_b), (0, step_a)):
            if 0 <= i - lag < len(order):
                step(i - lag)
    for at in live:
        for copy in at["back"]:
            copy.wait_recv()
        if "local" in at:
            at["local"].wait()
    combined = lax.dot_general(
        sel[...],
        slots[...].reshape(EXPERTS * PAIR, HALF),
        (((0,), (0,)), ((), ())),
        preferred_element_type=jnp.float32,
    )
    result[...] = combined.astype(jnp.bfloat16).reshape(2, TOK, HALF)
    last = net.send(result.at[1 - c], final, mate)
    last.wait_recv()

    @pl.when(c == 0)
    def _():
        out[:, 0:HALF] = result[0]
        out[:, HALF:QUARTER] = final[...]

    @pl.when(c == 1)
    def _():
        out[:, 0:HALF] = final[...]
        out[:, HALF:QUARTER] = result[1]

    net.finish()


def vmem():
    return pl.BlockSpec(memory_space=pltpu.VMEM)


def anywhere():
    return pl.BlockSpec(memory_space=pl.ANY)


def local(tokens, grad_out, routes, gates, w_up, w_down):
    bf16 = jnp.bfloat16
    xy, sel = pl.pallas_call(
        gather_kernel,
        out_shape=(
            jax.ShapeDtypeStruct((2, BLOCKS, PAIR, D), bf16),
            jax.ShapeDtypeStruct((EXPERTS * PAIR, 2 * TOK), bf16),
        ),
        in_specs=[vmem()] * 4,
        out_specs=(anywhere(), vmem()),
        scratch_shapes=[
            pltpu.VMEM((2, 2, TOK), jnp.int32),
            pltpu.VMEM((2, 2, TOK), jnp.float32),
            pltpu.VMEM((2, TOK, QUARTER), bf16),
            pltpu.VMEM((EXPERTS, PAIR, QUARTER), bf16),
            pltpu.SemaphoreType.DMA((110,)),
            pltpu.SemaphoreType.DMA((110,)),
            pltpu.SemaphoreType.DMA,
        ],
        compiler_params=pltpu.CompilerParams(collective_id=0, has_side_effects=True),
        name="gather_slots",
    )(routes.T, gates.T, tokens, grad_out)
    rows = xy.reshape(2, BLOCKS * PAIR, D)
    rows_x, rows_y = rows[0], rows[1]
    pre = jnp.dot(rows_x, w_up, preferred_element_type=jnp.float32)
    act = gelu_value(pre).astype(bf16)
    d_act = lax.dot_general(
        rows_y, w_down, (((1,), (1,)), ((), ())), preferred_element_type=jnp.float32
    )
    d_pre = (d_act * gelu_slope(pre)).astype(bf16)
    partial = lax.dot_general(
        d_pre, w_up, (((1,), (1,)), ((), ())), preferred_element_type=jnp.float32
    ).astype(bf16)
    grad_tokens = pl.pallas_call(
        return_kernel,
        out_shape=jax.ShapeDtypeStruct((TOK, QUARTER), bf16),
        in_specs=[vmem()] * 2,
        out_specs=vmem(),
        scratch_shapes=[
            pltpu.VMEM((4, BLOCKS, PAIR, HALF), bf16),
            pltpu.VMEM((4, BLOCKS, PAIR, HALF), bf16),
            pltpu.VMEM((Z, 2, 2, PAIR, HALF), bf16),
            pltpu.VMEM((Z, 2, 4, PAIR, HALF), bf16),
            pltpu.VMEM((Z, 2, PAIR, HALF), bf16),
            pltpu.VMEM((EXPERTS, PAIR, HALF), bf16),
            pltpu.VMEM((2, TOK, HALF), bf16),
            pltpu.VMEM((TOK, HALF), bf16),
            pltpu.SemaphoreType.DMA((100,)),
            pltpu.SemaphoreType.DMA((100,)),
            pltpu.SemaphoreType.DMA,
        ],
        compiler_params=pltpu.CompilerParams(
            collective_id=1, has_side_effects=True, vmem_limit_bytes=40 * 1024 * 1024
        ),
        name="return_slots",
    )(partial.reshape(BLOCKS, PAIR, D), sel)
    grad_up = lax.dot_general(
        rows_x, d_pre, (((0,), (0,)), ((), ())), preferred_element_type=jnp.float32
    )
    grad_down = lax.dot_general(
        act, rows_y, (((0,), (0,)), ((), ())), preferred_element_type=jnp.float32
    )
    return (grad_tokens, grad_up, grad_down)


def solution(mesh):
    return jax.shard_map(
        local,
        mesh=mesh,
        in_specs=(
            P("expert", "tensor"),
            P("expert", "tensor"),
            P("expert", None),
            P("expert", None),
            P(None, ("expert", "tensor")),
            P(("expert", "tensor"), None),
        ),
        out_specs=(
            P("expert", "tensor"),
            P(None, ("expert", "tensor")),
            P(("expert", "tensor"), None),
        ),
        check_vma=False,
    )
```

time: 407 us -> 171 us (0.42)
  blocking collectives: 137 us -> 0 us
  Pallas kernels: 0 us -> 136 us
  waiting for transfers between devices: 128 us -> 0 us
  local copies, waits for them, and re-layouts: 81 us -> 10.8 us
  starting transfers between devices: 14.1 us -> 0 us
  between operations: 14.3 us -> 0.73 us
  other arithmetic: 6.57 us -> 0.01 us
    all_to_all x2 -> x0, blocking collectives: 137 us -> none  [the longest x1 75.8 us: local(): lax.all_to_all(outgoing, 'expert', split_axis=1, concat_axis=1, tiled=True)]
    pallas_call x0 -> x2, Pallas kernels: none -> 136 us  [the longest x1 78.4 us: local(): pl.pallas_call(gather_kernel, out_shape=(jax.ShapeDtypeStruct((2, BLOCKS,...]
    all_gather x1 -> x0, waiting for transfers between devices: 102 us -> none  [local(): arrived = lax.all_gather(arrived, 'tensor', axis=3, tiled=True)]
    slice x2 -> x1, local copies, waits for them, and re-layouts: 52.6 us -> 10.1 us  [local(): rows_x, rows_y = (rows[0], rows[1])]
    all_to_all x1 -> x0, waiting for transfers between devices: 26.2 us -> none  [local(): lax.all_to_all(back.astype(jnp.bfloat16), 'expert', split_axis=0, concat_...]
    squeeze x2 -> x0, local copies, waits for them, and re-layouts: 18 us -> none  [the longest x1 9 us: local(): rows_y = rows[1]]
    all_to_all x1 -> x0, starting transfers between devices: 14.1 us -> none  [local(): lax.all_to_all(back.astype(jnp.bfloat16), 'expert', split_axis=0, concat_...]
    reduce_sum x4 -> x0, other arithmetic: 5.82 us -> none  [the longest x1 4.16 us: sum_at_owner(): return jnp.sum(tiles.astype(jnp.float32), axis=0)]
  transfers between devices with their start and end apart: 2 -> 0, of which waited for: 2 -> 0; matrix products, arithmetic and copies ran while one was open for 3% -> 0% of each run, Pallas kernels for 0% -> 0%
where the time goes in v1:
time: 171 us; the launch traced here: 168 us
  Pallas kernels  136 us (80%)
  matrix products  21.2 us (12%)
  local copies, waits for them, and re-layouts  10.8 us (6%)
    pallas_call x1, Pallas kernels, local(): pl.pallas_call(gather_kernel, out_shape=(jax.ShapeDtypeStruct((2, BLOCKS,...  78.4 us
    pallas_call x1, Pallas kernels, local(): pl.pallas_call(return_kernel, out_shape=jax.ShapeDtypeStruct((TOK, QUARTE...  57.1 us
    slice x1, local copies, waits for them, and re-layouts, local(): rows_x, rows_y = (rows[0], rows[1])  10.1 us
    dot_general x1, matrix products, local(): pre = jnp.dot(rows_x, w_up, preferred_element_type=jnp.float32)  5.13 us
    dot_general x1, matrix products, local(): lax.dot_general(act, rows_y, (((0,), (0,)), ((), ())), preferred_element_...  4.55 us
    dot_general x1, matrix products, local(): lax.dot_general(rows_x, d_pre, (((0,), (0,)), ((), ())), preferred_elemen...  4.48 us
    dot_general x1, matrix products, local(): lax.dot_general(rows_y, w_down, (((1,), (1,)), ((), ())), preferred_eleme...  3.87 us

profile of v1, /device:TPU:1, one launch (start us, length us, event | category | flops | bytes accessed | tf_op | source)
XLA Modules:
  0.0 168.2 jit_solution(1508373360559786493)
XLA Ops:
  0.6 0.0 copy-start
  0.6 78.4 %gather_slots.1 = (bf16[2,32,40,2048]{3,2,1,0:T(8,128)(2,1)}, bf16[640,256]{1,0:T(8,128)(2,1)}) custom-call(s32[2,128]{1,0:T(2,128)} %bitcast.21, f32[2,128]{1,0:T(2,128)} %bitcast.22, bf16[128,512]{1,0:T(8,128)(2,1)} %tok.1, bf16[128,512]{1,0:T(8,128)(2,1)} %grad.1), custom_call_target="tpu_custom_call" | custom-call | tf_op jit(solution)/shard_map/gather_slots/pallas_call | solution.py:373
  79.1 10.1 %fusion.8 = (bf16[1,32,40,2048]{3,2,1,0:T(8,128)(2,1)}, bf16[1,32,40,2048]{3,2,1,0:T(8,128)(2,1)}) fusion(bf16[2,32,40,2048]{3,2,1,0:T(8,128)(2,1)} %get-tuple-element.5), kind=kLoop, calls=%fused_computation.13 | loop fusion | bytes 20971520 | tf_op jit(solution)/shard_map/slice | solution.py:394
  89.2 0.0 copy-done
  89.2 0.0 copy-start.2
  89.2 0.0 copy-start.3
  89.2 0.0 slice-start
  89.2 5.1 %fusion.9 = f32[1280,512]{1,0:T(8,128)S(1)} fusion(bf16[1280,2048]{1,0:T(8,128)(2,1)} %bitcast.17, bf16[2048,512]{1,0:T(8,128)(2,1)S(1)} %copy-done), kind=kOutput, calls=%fused_computation.14 | convolution fusion | flops 2684354560 | bytes 9961472 | tf_op jit(solution)/shard_map/dot_general | solution.py:395
  94.3 0.0 copy-done.2
  94.3 0.0 copy-done.3
  94.4 0.0 slice-start.1
  94.4 3.9 %fusion = bf16[1280,512]{1,0:T(8,128)(2,1)S(1)} fusion(bf16[1280,2048]{1,0:T(8,128)(2,1)S(1)} %bitcast.15, bf16[512,2048]{1,0:T(8,128)(2,1)S(1)} %copy-done.3, f32[1280,512]{1,0:T(8,128)S(1)} %fusion.9), kind=kOutput, calls=%fused_computation.3 | convolution fusion | flops 2690908160 | bytes 11272192 | tf_op jit(solution)/shard_map/dot_general | solution.py:397
  98.2 4.6 %fusion.5 = f32[512,2048]{1,0:T(8,128)} fusion(bf16[1280,2048]{1,0:T(8,128)(2,1)S(1)} %bitcast.16, f32[1280,512]{1,0:T(8,128)S(1)} %fusion.9), kind=kOutput, calls=%fused_computation.10 | convolution fusion | flops 2687631360 | bytes 12058624 | tf_op jit(solution)/shard_map/dot_general | solution.py:430
  102.8 0.0 slice-done
  102.8 0.0 slice-done.1
  102.8 4.5 %fusion.10 = f32[2048,512]{1,0:T(8,128)} fusion(bf16[1280,2048]{1,0:T(8,128)(2,1)S(1)} %bitcast.20, bf16[1280,512]{1,0:T(8,128)(2,1)S(1)} %fusion), kind=kOutput, calls=%fused_computation.15 | convolution fusion | flops 2684354560 | bytes 10747904 | tf_op jit(solution)/shard_map/dot_general | solution.py:427
  107.3 0.0 copy-start.1
  107.3 3.1 %convolution_convert_fusion = bf16[1280,2048]{1,0:T(8,128)(2,1)S(1)} fusion(bf16[1280,512]{1,0:T(8,128)(2,1)S(1)} %fusion, bf16[2048,512]{1,0:T(8,128)(2,1)S(1)} %copy-done), kind=kOutput, calls=%fused_computation | convolution fusion | flops 2686976000 | bytes 8650752 | tf_op jit(solution)/shard_map/dot_general | solution.py:401
  110.4 0.0 copy-done.1
  110.4 57.1 %return_slots.1 = bf16[128,512]{1,0:T(8,128)(2,1)S(1)} custom-call(bf16[32,40,2048]{2,1,0:T(8,128)(2,1)S(1)} %bitcast.14, bf16[640,256]{1,0:T(8,128)(2,1)S(1)} %copy-done.1), custom_call_target="tpu_custom_call" | custom-call | tf_op jit(solution)/shard_map/return_slots/pallas_call | solution.py:404
  167.6 0.7 copy.10
  (1 shorter events, 0.0 us)
Async XLA Ops:
  0.6 88.6 %copy-start = (bf16[2048,512]{1,0:T(8,128)(2,1)S(1)}, bf16[2048,512]{1,0:T(8,128)(2,1)}, u32[]{:S(2)}) copy-start(bf16[2048,512]{1,0:T(8,128)(2,1)} %param.10) | copy-start | bytes 6291460
  89.2 5.2 %copy-start.2 = (bf16[1,32,40,2048]{3,2,1,0:T(8,128)(2,1)S(1)}, bf16[1,32,40,2048]{3,2,1,0:T(8,128)(2,1)}, u32[]{:S(2)}) copy-start(bf16[1,32,40,2048]{3,2,1,0:T(8,128)(2,1)} %get-tuple-element.8) | copy-start | bytes 15728644
  89.2 5.2 %copy-start.3 = (bf16[512,2048]{1,0:T(8,128)(2,1)S(1)}, bf16[512,2048]{1,0:T(8,128)(2,1)}, u32[]{:S(2)}) copy-start(bf16[512,2048]{1,0:T(8,128)(2,1)} %param.11) | copy-start | bytes 6291460
  89.2 13.6 %slice-start = ((s8[5242880]{0:T(1024)(128)(4,1)}), s8[4194304]{0:T(1024)(128)(4,1)S(1)}, s32[]{:S(2)}) async-start(s8[5242880]{0:T(1024)(128)(4,1)} %bitcast.18), calls=%async_computation | async-start | bytes 8388608
  94.4 8.4 %slice-start.1 = ((s8[5242880]{0:T(1024)(128)(4,1)}), s8[1048576]{0:T(1024)(128)(4,1)S(1)}, s32[]{:S(2)}) async-start(s8[5242880]{0:T(1024)(128)(4,1)} %bitcast.18), calls=%async_computation.1 | async-start | bytes 2097152
  107.3 3.1 %copy-start.1 = (bf16[640,256]{1,0:T(8,128)(2,1)S(1)}, bf16[640,256]{1,0:T(8,128)(2,1)}, u32[]{:S(2)}) copy-start(bf16[640,256]{1,0:T(8,128)(2,1)} %get-tuple-element.6.sel) | copy-start | bytes 983044

commit v2 on v0

v2 whole, which is shorter than its diff:
```python
import jax
import jax.numpy as jnp
from jax import lax
from jax.experimental import pallas as pl
from jax.experimental.pallas import tpu as pltpu
from jax.sharding import PartitionSpec as P

MESH = pl.DeviceIdType.MESH
Z, Y, X = 8, 4, 4
CAP, PAIR = 20, 40
EXPERTS = 16
BLOCKS = 32
ROWS = BLOCKS * PAIR
TOK = 128
QUARTER = 512
HALF = 256
D = 2048
HID_DEV = 512
TILE = 256
NEAR = (0, 1, 7, 2, 6, 3, 5, 4)
MODES = (0, 0, 1, 1, 1, 0, 0, 1)
RETURN_MODES = (0, 0, 0, 0, 0, 1, 1, 0)
GROUPS = ((0, 1), (2, 3), (4, 5), (6, 7))
ORDER = (
    "A0", "A1", "A2", "B0", "B1", "A3", "A4", "Br2", "Bl2", "Cr0", "Cl0", "A5", "A6", "Cr1", "Cl1",
    "Br3", "Bl3", "A7", "Br4", "Bl4", "C2", "B5", "D0", "B6", "D1", "C3", "F0", "C4", "Br7", "Bl7",
    "Cr5", "Cl5", "D2", "RA0", "Cr6", "Cl6", "RA1", "C7", "D3", "D5", "D4", "RB0", "F1", "RX0",
    "RB1", "RX1", "D6", "F2", "RA3", "RA2", "RC0", "D7", "RA4", "RC1", "RA5", "RB3", "RX3", "RD0",
    "RB2", "RX2", "F3", "RB4", "RX4", "RC3", "RD1", "GU0", "GD0", "RA6", "RY5", "RC2", "RA7", "GU1",
    "RD3", "GD1", "RC4", "GU2", "RB5", "RX5", "GD2", "RB7", "RX7", "GU3", "GD3", "GU4", "RY6",
    "RC5", "RD2", "GD4", "GU5", "RC7", "RD4", "GD5", "RB6", "RX6", "GU6", "GD6", "GU7", "RD7",
    "GD7", "RC6",
)

root_half = 0.7071067811865476
gauss_norm = 0.3989422804014327


def gelu_value(v):
    return 0.5 * v * (1.0 + lax.erf(v * root_half))


def gelu_slope(v):
    return 0.5 * (1.0 + lax.erf(v * root_half)) + v * jnp.exp(-0.5 * v * v) * gauss_norm


def place():
    e = lax.axis_index("expert")
    x = lax.axis_index("tensor")
    return e // 8, (e // 2) % 4, e % 2, x


def device(z, y, c, x):
    return ((z * Y + y) * 2 + c, x)


class Net:
    def __init__(self, send_sem, recv_sem):
        self.send_sem, self.recv_sem, self.count, self.sent = send_sem, recv_sem, 0, []

    def make(self, src, dst, target):
        i = self.count
        self.count += 1
        copy = pltpu.make_async_remote_copy(
            src_ref=src,
            dst_ref=dst,
            send_sem=self.send_sem.at[i],
            recv_sem=self.recv_sem.at[i],
            device_id=target,
            device_id_type=MESH,
        )
        self.sent.append(copy)
        return copy

    def send(self, src, dst, target):
        copy = self.make(src, dst, target)
        copy.start()
        return copy

    def finish(self):
        for copy in self.sent:
            copy.wait_send()


def kernel(
    routes, gates, tok, grad, w_up, w_down,
    out, grad_up, grad_down,
    route_buf, gate_buf, values, sel, send_slots, xy, wu, wd, act, d_pre, part, from_mate, acc,
    hop_a, hop_b, from_y, slots, result, final, tile_up, tile_down,
    send_sem, recv_sem, own_sem, tile_sem,
):
    z, y, c, x = place()
    k = ((y + 1) // 2) % 2
    partner = y + 1 - 2 * (y % 2)
    net = Net(send_sem, recv_sem)
    mate = device(z, y, 1 - c, x)
    right, left, far = (x + 1) % X, (x + 3) % X, (x + 2) % X
    to_right, to_left = device(z, y, c, right), device(z, y, c, left)
    to_y = device(z, partner, c, x)

    others = [mate, to_y, to_right, to_left]
    for dz in range(Z):
        for j in range(2):
            if dz or j:
                others.append(device((z + dz) % Z, y if j == 0 else 3 - y, c, x))
    barrier = pltpu.get_barrier_semaphore()
    for other in others:
        pl.semaphore_signal(barrier, inc=1, device_id=other, device_id_type=MESH)

    up_copy = pltpu.make_async_copy(w_up, wu, own_sem.at[0])
    down_copy = pltpu.make_async_copy(w_down, wd, own_sem.at[1])
    up_copy.start()
    down_copy.start()

    row = lax.broadcasted_iota(jnp.int32, (EXPERTS * PAIR, TOK), 0)
    expert = lax.broadcasted_iota(jnp.int32, (EXPERTS, TOK), 0)
    before = (
        lax.broadcasted_iota(jnp.int32, (TOK, TOK), 0)
        < lax.broadcasted_iota(jnp.int32, (TOK, TOK), 1)
    ).astype(jnp.bfloat16)

    def choose(r, g, s):
        named0 = (expert == r[0:1]).astype(jnp.float32)
        named1 = (expert == r[1:2]).astype(jnp.float32)
        earlier = jnp.dot(
            (named0 + named1).astype(jnp.bfloat16), before, preferred_element_type=jnp.float32
        )
        slot0 = jnp.sum(named0 * earlier, axis=0, keepdims=True).astype(jnp.int32)
        slot1 = jnp.sum(named1 * earlier, axis=0, keepdims=True).astype(jnp.int32)
        hit0 = row == r[0:1] * PAIR + s * CAP + slot0
        hit1 = row == r[1:2] * PAIR + s * CAP + slot1
        pick = jnp.where(hit0 | hit1, 1.0, 0.0).astype(jnp.bfloat16)
        weight = jnp.where(hit0, g[0:1], 0.0) + jnp.where(hit1, g[1:2], 0.0)
        return pick, jnp.sum(weight, axis=1, keepdims=True)

    mine = jnp.where(c == 0, tok[...], grad[...])
    pick, scale = choose(routes[...], gates[...], c)
    sel[c] = pick
    total = jnp.dot(pick, mine, preferred_element_type=jnp.float32)

    pl.semaphore_wait(barrier, len(others))
    first = net.send(routes, route_buf, mate)
    second = net.send(gates, gate_buf, mate)
    third = net.make(tok, values, mate)

    @pl.when(c == 0)
    def _():
        pltpu.make_async_remote_copy(
            src_ref=grad, dst_ref=values, send_sem=send_sem.at[2], recv_sem=recv_sem.at[2],
            device_id=mate, device_id_type=MESH,
        ).start()

    @pl.when(c == 1)
    def _():
        third.start()

    first.wait_recv()
    second.wait_recv()
    pick, more = choose(route_buf[...], gate_buf[...], 1 - c)
    sel[1 - c] = pick
    scale = scale + more
    third.wait_recv()
    total = total + jnp.dot(pick, values[...], preferred_element_type=jnp.float32)
    total = total * jnp.where(c == 0, 1.0, scale)
    send_slots[...] = total.astype(jnp.bfloat16).reshape(EXPERTS, PAIR, QUARTER)

    def cols(q, core=None):
        if core is None:
            return pl.ds(pl.multiple_of(q * QUARTER, QUARTER), QUARTER)
        return pl.ds(pl.multiple_of(q * QUARTER + core * HALF, HALF), HALF)

    ev = {}
    for n, dz in enumerate(NEAR):
        ze = (z + dz) % Z
        for j in range(2):
            src = send_slots.at[ze * 2 + (y // 2 if j == 0 else 1 - y // 2)]
            dst = xy.at[c, n * 4 + k * 2 + y // 2, :, cols(x)]
            if dz == 0 and j == 0:
                local_slots = pltpu.make_async_copy(src, dst, own_sem.at[2])
                local_slots.start()
            else:
                ev["z", n, j] = net.send(src, dst, device(ze, y if j == 0 else 3 - y, c, x))

    def share(key, block, count, q, target):
        ref = xy.at[c, pl.ds(block, count), :, cols(q)]
        ev[key] = net.send(ref, ref, target)

    def got(*keys):
        for key in keys:
            if key not in done:
                done.add(key)
                ev[key].wait_recv()

    done = set()

    def step_A(n):
        if n == 0:
            local_slots.wait()
        else:
            got(("z", n, 0))
        got(("z", n, 1))
        own = n * 4 + k * 2
        share(("r", n), own, 2, x, to_right)
        share(("l", n), own, 2, x, to_left)
        share(("y", n), own, 2, x, to_y)

    def step_B(n):
        got(("y", n))
        other = n * 4 + (1 - k) * 2
        share(("r2", n), other, 2, x, to_right)
        share(("l2", n), other, 2, x, to_left)

    def step_Cr(n):
        got(("r", n), ("r2", n))
        share(("fr", n), n * 4, 2, left, to_right)

    def step_Cl(n):
        got(("l", n), ("l2", n))
        share(("fl", n), n * 4 + 2, 2, right, to_left)

    def step_Br(n):
        got(("r", n))
        own = n * 4 + k * 2
        share(("fr", n), own, 1, left, to_right)
        share(("y1", n), own, 2, left, to_y)

    def step_Bl(n):
        got(("l", n))
        own = n * 4 + k * 2
        share(("fl", n), own + 1, 1, right, to_left)
        share(("y2", n), own, 2, right, to_y)

    def step_C(n):
        got(("fr", n), ("fl", n))
        share(("y3", n), n * 4 + k * 2, 2, far, to_y)

    def step_D(n):
        if MODES[n]:
            got(("y", n), ("y1", n), ("y2", n), ("y3", n))
        else:
            got(("fr", n), ("fl", n))
        ref = xy.at[c, pl.ds(n * 4, 4)]
        ev["m", n] = net.send(ref, ref, mate)

    def step_F(g):
        if g == 0:
            up_copy.wait()
            down_copy.wait()
        got(*[("m", n) for n in GROUPS[g]])
        first_block, count = GROUPS[g][0] * 4, len(GROUPS[g]) * 4
        rows, size = pl.ds(first_block * PAIR, count * PAIR), count * PAIR
        rows_x = xy[0, pl.ds(first_block, count)].reshape(size, D)
        rows_y = xy[1, pl.ds(first_block, count)].reshape(size, D)
        pre = jnp.dot(rows_x, wu[...], preferred_element_type=jnp.float32)
        d_act = lax.dot_general(
            rows_y, wd[...], (((1,), (1,)), ((), ())), preferred_element_type=jnp.float32
        )
        act[rows] = gelu_value(pre).astype(jnp.bfloat16)
        slope = (d_act * gelu_slope(pre)).astype(jnp.bfloat16)
        d_pre[rows] = slope
        product = lax.dot_general(
            slope, wu[...], (((1,), (1,)), ((), ())), preferred_element_type=jnp.float32
        )
        part[pl.ds(first_block, count)] = product.astype(jnp.bfloat16).reshape(count, PAIR, D)
        for n in GROUPS[g]:
            for q in range(4):
                ev["p", n, q] = net.send(
                    part.at[pl.ds(n * 4, 4), :, cols(q, 1 - c)], from_mate.at[q, pl.ds(n * 4, 4)], mate
                )

    def wide(value):
        return value.astype(jnp.float32)

    def add(ref, other):
        ref[...] = (wide(ref[...]) + wide(other[...])).astype(jnp.bfloat16)

    def step_RA(n):
        for q in range(4):
            got(("p", n, q))
            acc[q, pl.ds(n * 4, 4)] = (
                wide(part[pl.ds(n * 4, 4), :, cols(q, c)]) + wide(from_mate[q, pl.ds(n * 4, 4)])
            ).astype(jnp.bfloat16)
        if RETURN_MODES[n]:
            ev["ry", n] = net.send(
                acc.at[pl.ds(0, 4), pl.ds(n * 4 + (1 - k) * 2, 2)], from_y.at[n], to_y
            )
        else:
            ev["ar", n] = net.send(acc.at[far, pl.ds(n * 4, 2)], hop_a.at[n, 0], to_right)
            ev["al", n] = net.send(acc.at[far, pl.ds(n * 4 + 2, 2)], hop_a.at[n, 1], to_left)

    def step_RY(n):
        got(("ry", n))
        own = n * 4 + k * 2
        add(acc.at[pl.ds(0, 4), pl.ds(own, 2)], from_y.at[n])
        ev["ar", n] = net.send(acc.at[far, pl.ds(own, 1)], hop_a.at[n, 0, pl.ds(0, 1)], to_right)
        ev["al", n] = net.send(acc.at[far, pl.ds(own + 1, 1)], hop_a.at[n, 1, pl.ds(0, 1)], to_left)

    def step_RB(n):
        got(("ar", n))
        if RETURN_MODES[n]:
            own = n * 4 + k * 2
            add(acc.at[right, pl.ds(own, 1)], hop_a.at[n, 0, pl.ds(0, 1)])
            ev["br", n] = net.send(acc.at[right, pl.ds(own, 2)], hop_b.at[n, 0, pl.ds(0, 2)], to_right)
        else:
            add(acc.at[right, pl.ds(n * 4, 2)], hop_a.at[n, 0])
            ev["br", n] = net.send(acc.at[right, pl.ds(n * 4, 4)], hop_b.at[n, 0], to_right)

    def step_RX(n):
        got(("al", n))
        if RETURN_MODES[n]:
            own = n * 4 + k * 2
            add(acc.at[left, pl.ds(own + 1, 1)], hop_a.at[n, 1, pl.ds(0, 1)])
            ev["bl", n] = net.send(acc.at[left, pl.ds(own, 2)], hop_b.at[n, 1, pl.ds(0, 2)], to_left)
        else:
            add(acc.at[left, pl.ds(n * 4 + 2, 2)], hop_a.at[n, 1])
            ev["bl", n] = net.send(acc.at[left, pl.ds(n * 4, 4)], hop_b.at[n, 1], to_left)

    def step_RC(n):
        got(("br", n), ("bl", n))
        block, count = (n * 4 + k * 2, 2) if RETURN_MODES[n] else (n * 4, 4)
        ref = acc.at[x, pl.ds(block, count)]
        ref[...] = (
            wide(ref[...]) + wide(hop_b[n, 0, pl.ds(0, count)]) + wide(hop_b[n, 1, pl.ds(0, count)])
        ).astype(jnp.bfloat16)
        if RETURN_MODES[n]:
            give_back(n)
        else:
            ev["ry", n] = net.send(
                acc.at[x, pl.ds(n * 4 + (1 - k) * 2, 2)], from_y.at[n, 0], to_y
            )

    def step_RD(n):
        got(("ry", n))
        add(acc.at[x, pl.ds(n * 4 + k * 2, 2)], from_y.at[n, 0])
        give_back(n)

    me = z * 2 + y // 2

    def give_back(n):
        zs = (z + Z - NEAR[n]) % Z
        for j in range(2):
            src = acc.at[x, n * 4 + k * 2 + (y // 2 if j == 0 else 1 - y // 2)]
            if n == 0 and j == 0:
                ev["own_back"] = pltpu.make_async_copy(src, slots.at[me], own_sem.at[3])
                ev["own_back"].start()
            else:
                ev["back", n, j] = net.send(
                    src, slots.at[me], device(zs, y if j == 0 else 3 - y, c, x)
                )

    stores = {"GU": [], "GD": []}

    def store(name, i, src, dst):
        copy = pltpu.make_async_copy(src, dst, tile_sem.at[0 if name == "GU" else 1, i % 2])
        copy.start()
        stores[name].append(copy)

    def step_GU(i):
        if i >= 2:
            stores["GU"][i - 2].wait()
        tile = xy[0, :, :, i * TILE : (i + 1) * TILE].reshape(ROWS, TILE)
        tile_up[i % 2] = lax.dot_general(
            tile, d_pre[...], (((0,), (0,)), ((), ())), preferred_element_type=jnp.float32
        )
        store("GU", i, tile_up.at[i % 2], grad_up.at[pl.ds(i * TILE, TILE)])

    def step_GD(i):
        if i >= 2:
            stores["GD"][i - 2].wait()
        tile = xy[1, :, :, i * TILE : (i + 1) * TILE].reshape(ROWS, TILE)
        tile_down[i % 2] = lax.dot_general(
            act[...], tile, (((0,), (0,)), ((), ())), preferred_element_type=jnp.float32
        )
        store("GD", i, tile_down.at[i % 2], grad_down.at[:, pl.ds(i * TILE, TILE)])

    steps = dict(
        A=step_A, B=step_B, Br=step_Br, Bl=step_Bl, Cr=step_Cr, Cl=step_Cl, C=step_C, D=step_D,
        F=step_F, RA=step_RA, RY=step_RY, RB=step_RB, RX=step_RX, RC=step_RC, RD=step_RD,
        GU=step_GU, GD=step_GD,
    )
    for name in ORDER:
        steps[name[:-1]](int(name[-1]))

    for key in list(ev):
        if key[0] == "back":
            got(key)
    ev["own_back"].wait()
    combined = jnp.zeros((2 * TOK, HALF), jnp.float32)
    back = slots[...].reshape(EXPERTS * PAIR, HALF)

    def combine(s):
        return lax.dot_general(
            sel[s], back, (((0,), (0,)), ((), ())), preferred_element_type=jnp.float32
        ).astype(jnp.bfloat16)

    result[0] = combine(1 - c)
    last = net.send(result.at[0], final, mate)
    result[1] = combine(c)
    last.wait_recv()

    @pl.when(c == 0)
    def _():
        out[:, 0:HALF] = result[1]
        out[:, HALF:QUARTER] = final[...]

    @pl.when(c == 1)
    def _():
        out[:, 0:HALF] = final[...]
        out[:, HALF:QUARTER] = result[1]

    for name in ("GU", "GD"):
        for copy in stores[name][-2:]:
            copy.wait()
    net.finish()


def local(tokens, grad_out, routes, gates, w_up, w_down):
    bf16, f32 = jnp.bfloat16, jnp.float32
    inside = pl.BlockSpec(memory_space=pltpu.VMEM)
    anywhere = pl.BlockSpec(memory_space=pl.ANY)
    return pl.pallas_call(
        kernel,
        out_shape=(
            jax.ShapeDtypeStruct((TOK, QUARTER), bf16),
            jax.ShapeDtypeStruct((D, HID_DEV), f32),
            jax.ShapeDtypeStruct((HID_DEV, D), f32),
        ),
        in_specs=[inside] * 4 + [anywhere] * 2,
        out_specs=(inside, anywhere, anywhere),
        scratch_shapes=[
            pltpu.VMEM((2, TOK), jnp.int32),
            pltpu.VMEM((2, TOK), f32),
            pltpu.VMEM((TOK, QUARTER), bf16),
            pltpu.VMEM((2, EXPERTS * PAIR, TOK), bf16),
            pltpu.VMEM((EXPERTS, PAIR, QUARTER), bf16),
            pltpu.VMEM((2, BLOCKS, PAIR, D), bf16),
            pltpu.VMEM((D, HID_DEV), bf16),
            pltpu.VMEM((HID_DEV, D), bf16),
            pltpu.VMEM((ROWS, HID_DEV), bf16),
            pltpu.VMEM((ROWS, HID_DEV), bf16),
            pltpu.VMEM((BLOCKS, PAIR, D), bf16),
            pltpu.VMEM((4, BLOCKS, PAIR, HALF), bf16),
            pltpu.VMEM((4, BLOCKS, PAIR, HALF), bf16),
            pltpu.VMEM((Z, 2, 2, PAIR, HALF), bf16),
            pltpu.VMEM((Z, 2, 4, PAIR, HALF), bf16),
            pltpu.VMEM((Z, 4, 2, PAIR, HALF), bf16),
            pltpu.VMEM((EXPERTS, PAIR, HALF), bf16),
            pltpu.VMEM((2, TOK, HALF), bf16),
            pltpu.VMEM((TOK, HALF), bf16),
            pltpu.VMEM((2, TILE, HID_DEV), f32),
            pltpu.VMEM((2, HID_DEV, TILE), f32),
            pltpu.SemaphoreType.DMA((224,)),
            pltpu.SemaphoreType.DMA((224,)),
            pltpu.SemaphoreType.DMA((4,)),
            pltpu.SemaphoreType.DMA((2, 2)),
        ],
        compiler_params=pltpu.CompilerParams(
            collective_id=0, has_side_effects=True, vmem_limit_bytes=60 * 1024 * 1024
        ),
        name="expert_backward",
    )(routes.T, gates.T, tokens, grad_out, w_up, w_down)


def solution(mesh):
    return jax.shard_map(
        local,
        mesh=mesh,
        in_specs=(
            P("expert", "tensor"),
            P("expert", "tensor"),
            P("expert", None),
            P("expert", None),
            P(None, ("expert", "tensor")),
            P(("expert", "tensor"), None),
        ),
        out_specs=(
            P("expert", "tensor"),
            P(None, ("expert", "tensor")),
            P(("expert", "tensor"), None),
        ),
        check_vma=False,
    )
```

time: 407 us -> 102 us (0.25)
  blocking collectives: 137 us -> 0 us
  waiting for transfers between devices: 128 us -> 0 us
  Pallas kernels: 0 us -> 92.4 us
  local copies, waits for them, and re-layouts: 81 us -> 8.4 us
  matrix products: 25.2 us -> 0 us
  starting transfers between devices: 14.1 us -> 0 us
  between operations: 14.3 us -> 0.64 us
  other arithmetic: 6.57 us -> 0 us
    all_to_all x2 -> x0, blocking collectives: 137 us -> none  [the longest x1 75.8 us: local(): lax.all_to_all(outgoing, 'expert', split_axis=1, concat_axis=1, tiled=True)]
    all_gather x1 -> x0, waiting for transfers between devices: 102 us -> none  [local(): arrived = lax.all_gather(arrived, 'tensor', axis=3, tiled=True)]
    pallas_call x0 -> x1, Pallas kernels: none -> 92.4 us  [local(): pl.pallas_call(kernel, out_shape=(jax.ShapeDtypeStruct((TOK, QUARTER), bf...]
    slice x2 -> x0, local copies, waits for them, and re-layouts: 52.6 us -> none  [the longest x1 52.4 us: local(): rows_x = rows[0]]
    all_to_all x1 -> x0, waiting for transfers between devices: 26.2 us -> none  [local(): lax.all_to_all(back.astype(jnp.bfloat16), 'expert', split_axis=0, concat_...]
    dot_general x7 -> x0, matrix products: 25.2 us -> none  [the longest x1 7.96 us: local(): lax.dot_general(rows_x, d_pre, (((0,), (0,)), ((), ())), preferred_elemen...]
    squeeze x2 -> x0, local copies, waits for them, and re-layouts: 18 us -> none  [the longest x1 9 us: local(): rows_y = rows[1]]
    all_to_all x1 -> x0, starting transfers between devices: 14.1 us -> none  [local(): lax.all_to_all(back.astype(jnp.bfloat16), 'expert', split_axis=0, concat_...]
  transfers between devices with their start and end apart: 2 -> 0, of which waited for: 2 -> 0; matrix products, arithmetic and copies ran while one was open for 3% -> 0% of each run, Pallas kernels for 0% -> 0%
where the time goes in v2:
time: 102 us; the launch traced here: 101 us
  Pallas kernels  92.4 us (91%)
  local copies, waits for them, and re-layouts  8.4 us (8%)
    pallas_call x1, Pallas kernels, local(): pl.pallas_call(kernel, out_shape=(jax.ShapeDtypeStruct((TOK, QUARTER), bf...  92.4 us
    unnamed x5, local copies, waits for them, and re-layouts  8.4 us

profile of v2, /device:TPU:1, one launch (start us, length us, event | category | flops | bytes accessed | tf_op | source)
XLA Modules:
  0.0 101.5 jit_solution(17001622024765826710)
XLA Ops:
  0.6 92.4 %expert_backward.1 = (bf16[128,512]{1,0:T(8,128)(2,1)}, f32[2048,512]{1,0:T(8,128)}, f32[512,2048]{1,0:T(8,128)}) custom-call(s32[2,128]{1,0:T(2,128)} %bitcast.2, f32[2,128]{1,0:T(2,128)} %bitcast.3, bf16[128,512]{1,0:T(8,128)(2,1)} %tok.1, bf16[128,512]{1,0:T(8,128)(2,1)} %grad.1, bf16[2048,512]{1,0:T(8,128)(2,1)} %w_up.1, bf16[512,2048]{1,0:T(8,128)(2,1)} %w_down.1), custom_call_target="tpu_custom_call" | custom-call | tf_op jit(solution)/shard_map/expert_backward/pallas_call | solution.py:421
  93.1 1.6 %copy.12 = bf16[128,512]{1,0:T(8,128)(2,1)} copy(bf16[128,512]{1,0:T(8,128)(2,1)} %get-tuple-element.6) | data formatting | bytes 262144
  94.6 0.0 copy-start
  94.6 4.8 %copy.13 = f32[2048,512]{1,0:T(8,128)} copy(f32[2048,512]{1,0:T(8,128)} %get-tuple-element.7) | data formatting | bytes 8388608
  99.5 0.0 copy-done
  99.5 2.0 %copy.14 = f32[512,2048]{1,0:T(8,128)} copy(f32[512,2048]{1,0:T(8,128)S(1)} %copy-done) | data formatting | bytes 8388608
Async XLA Ops:
  94.6 4.8 %copy-start = (f32[512,2048]{1,0:T(8,128)S(1)}, f32[512,2048]{1,0:T(8,128)}, u32[]{:S(2)}) copy-start(f32[512,2048]{1,0:T(8,128)} %get-tuple-element.8) | copy-start | bytes 12582916

commit v3 on v2

--- a/solution.py
+++ b/solution.py
@@ -17,19 +17,20 @@
 D = 2048
 HID_DEV = 512
 TILE = 256
+PARTS = 4
+VMEM_MIB = 46
 NEAR = (0, 1, 7, 2, 6, 3, 5, 4)
-MODES = (0, 0, 1, 1, 1, 0, 0, 1)
-RETURN_MODES = (0, 0, 0, 0, 0, 1, 1, 0)
+MODES = (1, 0, 0, 1, 0, 0, 1, 0)
+RETURN_MODES = (1, 0, 1, 0, 1, 0, 0, 0)
 GROUPS = ((0, 1), (2, 3), (4, 5), (6, 7))
 ORDER = (
-    "A0", "A1", "A2", "B0", "B1", "A3", "A4", "Br2", "Bl2", "Cr0", "Cl0", "A5", "A6", "Cr1", "Cl1",
-    "Br3", "Bl3", "A7", "Br4", "Bl4", "C2", "B5", "D0", "B6", "D1", "C3", "F0", "C4", "Br7", "Bl7",
-    "Cr5", "Cl5", "D2", "RA0", "Cr6", "Cl6", "RA1", "C7", "D3", "D5", "D4", "RB0", "F1", "RX0",
-    "RB1", "RX1", "D6", "F2", "RA3", "RA2", "RC0", "D7", "RA4", "RC1", "RA5", "RB3", "RX3", "RD0",
-    "RB2", "RX2", "F3", "RB4", "RX4", "RC3", "RD1", "GU0", "GD0", "RA6", "RY5", "RC2", "RA7", "GU1",
-    "RD3", "GD1", "RC4", "GU2", "RB5", "RX5", "GD2", "RB7", "RX7", "GU3", "GD3", "GU4", "RY6",
-    "RC5", "RD2", "GD4", "GU5", "RC7", "RD4", "GD5", "RB6", "RX6", "GU6", "GD6", "GU7", "RD7",
-    "GD7", "RC6",
+    "A0", "A1", "A2", "Br0", "Bl0", "B1", "A3", "A4", "B2", "C0", "Cr1", "Cl1", "Br3", "Bl3", "A5",
+    "A6", "B4", "Cr2", "Cl2", "A7", "D0", "D1", "C3", "F0", "B5", "Br6", "Bl6", "Cr4", "Cl4", "RA0",
+    "D2", "B7", "RA1", "D3", "Cr5", "Cl5", "F1", "D4", "C6", "Cr7", "Cl7", "RA2", "RY0", "RB1",
+    "RX1", "RA3", "D5", "D6", "D7", "RB0", "RX0", "F2", "RC1", "RY2", "RB3", "RX3", "F3", "RC0",
+    "RB2", "RX2", "RA4", "RA5", "GU0", "RC3", "RA6", "GD0", "RA7", "RC2", "GU1", "RB5", "RX5",
+    "GD1", "GU2", "RB6", "RX6", "GD2", "RY4", "RB7", "RX7", "GU3", "GD3", "RC5", "GU4", "GD4",
+    "GU5", "RB4", "RX4", "RC6", "GD5", "GU6", "GD6", "RC7", "GU7", "RC4", "GD7",
 )
 
 root_half = 0.7071067811865476
@@ -86,8 +87,8 @@
     routes, gates, tok, grad, w_up, w_down,
     out, grad_up, grad_down,
     route_buf, gate_buf, values, sel, send_slots, xy, wu, wd, act, d_pre, part, from_mate, acc,
-    hop_a, hop_b, from_y, slots, result, final, tile_up, tile_down,
-    send_sem, recv_sem, own_sem, tile_sem,
+    hop_a, hop_b, from_y, slots, result, final,
+    send_sem, recv_sem, own_sem,
 ):
     z, y, c, x = place()
     k = ((y + 1) // 2) % 2
@@ -98,11 +99,12 @@
     to_right, to_left = device(z, y, c, right), device(z, y, c, left)
     to_y = device(z, partner, c, x)
 
-    others = [mate, to_y, to_right, to_left]
-    for dz in range(Z):
-        for j in range(2):
-            if dz or j:
-                others.append(device((z + dz) % Z, y if j == 0 else 3 - y, c, x))
+    slots[...] = jnp.zeros_like(slots)
+    others = [mate, to_right, to_left]
+    for dz in NEAR[::-1]:
+        for row in (3 - partner, 3 - y, partner, y):
+            if dz or row is not y:
+                others.append(device((z + dz) % Z, row, c, x))
     barrier = pltpu.get_barrier_semaphore()
     for other in others:
         pl.semaphore_signal(barrier, inc=1, device_id=other, device_id_type=MESH)
@@ -315,67 +317,46 @@
             add(acc.at[left, pl.ds(n * 4 + 2, 2)], hop_a.at[n, 1])
             ev["bl", n] = net.send(acc.at[left, pl.ds(n * 4, 4)], hop_b.at[n, 1], to_left)
 
+    me = z * 2 + y // 2
+
     def step_RC(n):
         got(("br", n), ("bl", n))
-        block, count = (n * 4 + k * 2, 2) if RETURN_MODES[n] else (n * 4, 4)
+        own = n * 4 + k * 2
+        block, count = (own, 2) if RETURN_MODES[n] else (n * 4, 4)
         ref = acc.at[x, pl.ds(block, count)]
         ref[...] = (
             wide(ref[...]) + wide(hop_b[n, 0, pl.ds(0, count)]) + wide(hop_b[n, 1, pl.ds(0, count)])
         ).astype(jnp.bfloat16)
-        if RETURN_MODES[n]:
-            give_back(n)
-        else:
-            ev["ry", n] = net.send(
-                acc.at[x, pl.ds(n * 4 + (1 - k) * 2, 2)], from_y.at[n, 0], to_y
-            )
-
-    def step_RD(n):
-        got(("ry", n))
-        add(acc.at[x, pl.ds(n * 4 + k * 2, 2)], from_y.at[n, 0])
-        give_back(n)
-
-    me = z * 2 + y // 2
-
-    def give_back(n):
         zs = (z + Z - NEAR[n]) % Z
-        for j in range(2):
-            src = acc.at[x, n * 4 + k * 2 + (y // 2 if j == 0 else 1 - y // 2)]
+        other = n * 4 + (1 - k) * 2
+        for j in range(2 if RETURN_MODES[n] else 4):
+            row = y if j % 2 == 0 else 3 - y
+            block = own if j < 2 else other
+            block = block + (y // 2 if j % 2 == 0 else 1 - y // 2)
+            if j >= 2:
+                row = partner if j % 2 == 0 else 3 - partner
+            dst = slots.at[j // 2, me]
             if n == 0 and j == 0:
-                ev["own_back"] = pltpu.make_async_copy(src, slots.at[me], own_sem.at[3])
+                ev["own_back"] = pltpu.make_async_copy(acc.at[x, block], dst, own_sem.at[3])
                 ev["own_back"].start()
             else:
-                ev["back", n, j] = net.send(
-                    src, slots.at[me], device(zs, y if j == 0 else 3 - y, c, x)
-                )
-
-    stores = {"GU": [], "GD": []}
-
-    def store(name, i, src, dst):
-        copy = pltpu.make_async_copy(src, dst, tile_sem.at[0 if name == "GU" else 1, i % 2])
-        copy.start()
-        stores[name].append(copy)
+                ev["back", n, j] = net.send(acc.at[x, block], dst, device(zs, row, c, x))
 
     def step_GU(i):
-        if i >= 2:
-            stores["GU"][i - 2].wait()
         tile = xy[0, :, :, i * TILE : (i + 1) * TILE].reshape(ROWS, TILE)
-        tile_up[i % 2] = lax.dot_general(
+        grad_up[i * TILE : (i + 1) * TILE] = lax.dot_general(
             tile, d_pre[...], (((0,), (0,)), ((), ())), preferred_element_type=jnp.float32
         )
-        store("GU", i, tile_up.at[i % 2], grad_up.at[pl.ds(i * TILE, TILE)])
 
     def step_GD(i):
-        if i >= 2:
-            stores["GD"][i - 2].wait()
         tile = xy[1, :, :, i * TILE : (i + 1) * TILE].reshape(ROWS, TILE)
-        tile_down[i % 2] = lax.dot_general(
+        grad_down[:, i * TILE : (i + 1) * TILE] = lax.dot_general(
             act[...], tile, (((0,), (0,)), ((), ())), preferred_element_type=jnp.float32
         )
-        store("GD", i, tile_down.at[i % 2], grad_down.at[:, pl.ds(i * TILE, TILE)])
 
     steps = dict(
         A=step_A, B=step_B, Br=step_Br, Bl=step_Bl, Cr=step_Cr, Cl=step_Cl, C=step_C, D=step_D,
-        F=step_F, RA=step_RA, RY=step_RY, RB=step_RB, RX=step_RX, RC=step_RC, RD=step_RD,
+        F=step_F, RA=step_RA, RY=step_RY, RB=step_RB, RX=step_RX, RC=step_RC,
         GU=step_GU, GD=step_GD,
     )
     for name in ORDER:
@@ -385,13 +366,16 @@
         if key[0] == "back":
             got(key)
     ev["own_back"].wait()
-    combined = jnp.zeros((2 * TOK, HALF), jnp.float32)
-    back = slots[...].reshape(EXPERTS * PAIR, HALF)
-
     def combine(s):
-        return lax.dot_general(
-            sel[s], back, (((0,), (0,)), ((), ())), preferred_element_type=jnp.float32
-        ).astype(jnp.bfloat16)
+        total = jnp.zeros((TOK, HALF), jnp.float32)
+        for h in range(2):
+            total = total + lax.dot_general(
+                sel[s],
+                slots[h].reshape(EXPERTS * PAIR, HALF),
+                (((0,), (0,)), ((), ())),
+                preferred_element_type=jnp.float32,
+            )
+        return total.astype(jnp.bfloat16)
 
     result[0] = combine(1 - c)
     last = net.send(result.at[0], final, mate)
@@ -408,25 +392,35 @@
         out[:, 0:HALF] = final[...]
         out[:, HALF:QUARTER] = result[1]
 
-    for name in ("GU", "GD"):
-        for copy in stores[name][-2:]:
-            copy.wait()
     net.finish()
+
+
+def store_kernel(tok, up, down, tok_out, up_out, down_out, sem):
+    copies = [pltpu.make_async_copy(tok, tok_out, sem.at[0])]
+    for i in range(PARTS):
+        for j, (src, dst) in enumerate(((up, up_out), (down, down_out))):
+            size = src.shape[0] // PARTS
+            rows = pl.ds(i * size, size)
+            copies.append(pltpu.make_async_copy(src.at[rows], dst.at[rows], sem.at[1 + 2 * i + j]))
+    for copy in copies:
+        copy.start()
+    for copy in copies:
+        copy.wait()
 
 
 def local(tokens, grad_out, routes, gates, w_up, w_down):
     bf16, f32 = jnp.bfloat16, jnp.float32
     inside = pl.BlockSpec(memory_space=pltpu.VMEM)
     anywhere = pl.BlockSpec(memory_space=pl.ANY)
-    return pl.pallas_call(
+    grads = pl.pallas_call(
         kernel,
         out_shape=(
-            jax.ShapeDtypeStruct((TOK, QUARTER), bf16),
-            jax.ShapeDtypeStruct((D, HID_DEV), f32),
-            jax.ShapeDtypeStruct((HID_DEV, D), f32),
+            pltpu.VMEM((TOK, QUARTER), bf16),
+            pltpu.VMEM((D, HID_DEV), f32),
+            pltpu.VMEM((HID_DEV, D), f32),
         ),
         in_specs=[inside] * 4 + [anywhere] * 2,
-        out_specs=(inside, anywhere, anywhere),
+        out_specs=(inside, inside, inside),
         scratch_shapes=[
             pltpu.VMEM((2, TOK), jnp.int32),
             pltpu.VMEM((2, TOK), f32),
@@ -444,21 +438,27 @@
             pltpu.VMEM((Z, 2, 2, PAIR, HALF), bf16),
             pltpu.VMEM((Z, 2, 4, PAIR, HALF), bf16),
             pltpu.VMEM((Z, 4, 2, PAIR, HALF), bf16),
-            pltpu.VMEM((EXPERTS, PAIR, HALF), bf16),
+            pltpu.VMEM((2, EXPERTS, PAIR, HALF), bf16),
             pltpu.VMEM((2, TOK, HALF), bf16),
             pltpu.VMEM((TOK, HALF), bf16),
-            pltpu.VMEM((2, TILE, HID_DEV), f32),
-            pltpu.VMEM((2, HID_DEV, TILE), f32),
             pltpu.SemaphoreType.DMA((224,)),
             pltpu.SemaphoreType.DMA((224,)),
             pltpu.SemaphoreType.DMA((4,)),
-            pltpu.SemaphoreType.DMA((2, 2)),
         ],
         compiler_params=pltpu.CompilerParams(
-            collective_id=0, has_side_effects=True, vmem_limit_bytes=60 * 1024 * 1024
+            collective_id=0, has_side_effects=True, vmem_limit_bytes=VMEM_MIB * 1024 * 1024
         ),
         name="expert_backward",
     )(routes.T, gates.T, tokens, grad_out, w_up, w_down)
+    return pl.pallas_call(
+        store_kernel,
+        out_shape=tuple(jax.ShapeDtypeStruct(g.shape, g.dtype) for g in grads),
+        in_specs=[inside] * 3,
+        out_specs=(anywhere,) * 3,
+        scratch_shapes=[pltpu.SemaphoreType.DMA((1 + 2 * PARTS,))],
+        compiler_params=pltpu.CompilerParams(vmem_limit_bytes=1024 * 1024),
+        name="store_grads",
+    )(*grads)
 
 
 def solution(mesh):

time: 102 us -> 95.2 us (0.933)
  local copies, waits for them, and re-layouts: 8.4 us -> 0 us
  Pallas kernels: 92.4 us -> 94.3 us
    unnamed x5 -> x0, local copies, waits for them, and re-layouts: 8.4 us -> none
    pallas_call x1 -> x2, Pallas kernels: 92.4 us -> 94.3 us  [the longest x1 90.9 us: local(): pl.pallas_call(kernel, out_shape=(pltpu.VMEM((TOK, QUARTER), bf16), pltpu...]
where the time goes in v3:
time: 95.2 us; the launch traced here: 95.1 us
  Pallas kernels  94.3 us (99%)
    pallas_call x1, Pallas kernels, local(): pl.pallas_call(kernel, out_shape=(pltpu.VMEM((TOK, QUARTER), bf16), pltpu...  90.9 us
    pallas_call x1, Pallas kernels, local(): pl.pallas_call(store_kernel, out_shape=tuple((jax.ShapeDtypeStruct(g.shap...  3.42 us

profile of v3, /device:TPU:1, one launch (start us, length us, event | category | flops | bytes accessed | tf_op | source)
XLA Modules:
  0.0 95.1 jit_solution(5076705134864204362)
XLA Ops:
  0.6 90.9 %expert_backward.1 = (bf16[128,512]{1,0:T(8,128)(2,1)S(1)}, f32[2048,512]{1,0:T(8,128)S(1)}, f32[512,2048]{1,0:T(8,128)S(1)}) custom-call(s32[2,128]{1,0:T(2,128)} %bitcast.2, f32[2,128]{1,0:T(2,128)} %bitcast.3, bf16[128,512]{1,0:T(8,128)(2,1)} %tok.1, bf16[128,512]{1,0:T(8,128)(2,1)} %grad.1, bf16[2048,512]{1,0:T(8,128)(2,1)} %w_up.1, bf16[512,2048]{1,0:T(8,128)(2,1)} %w_down.1), custom_call_target="tpu_custom_call" | custom-call | tf_op jit(solution)/shard_map/expert_backward/pallas_call | solution.py:415
  91.6 3.4 %store_grads.1 = (bf16[128,512]{1,0:T(8,128)(2,1)}, f32[2048,512]{1,0:T(8,128)}, f32[512,2048]{1,0:T(8,128)}) custom-call(bf16[128,512]{1,0:T(8,128)(2,1)S(1)} %get-tuple-element.6.tok, f32[2048,512]{1,0:T(8,128)S(1)} %get-tuple-element.7.up, f32[512,2048]{1,0:T(8,128)S(1)} %get-tuple-element.8.down), custom_call_target="tpu_custom_call" | custom-call | tf_op jit(solution)/shard_map/store_grads/pallas_call | solution.py:453

commit v4 on v3

--- a/solution.py
+++ b/solution.py
@@ -17,20 +17,20 @@
 D = 2048
 HID_DEV = 512
 TILE = 256
-PARTS = 4
-VMEM_MIB = 46
-NEAR = (0, 1, 7, 2, 6, 3, 5, 4)
-MODES = (1, 0, 0, 1, 0, 0, 1, 0)
-RETURN_MODES = (1, 0, 1, 0, 1, 0, 0, 0)
-GROUPS = ((0, 1), (2, 3), (4, 5), (6, 7))
+PARTS = 1
+VMEM_MIB = 48
+NEAR = (0, 7, 2, 6, 4, 3, 5, 1)
+MODES = (1, 0, 1, 0, 0, 1, 1, 0)
+RETURN_MODES = (0, 0, 2, 1, 0, 0, 1, 0)
+GROUPS = ((0, 1), (2, 3), (4, 5), (6,), (7,))
 ORDER = (
-    "A0", "A1", "A2", "Br0", "Bl0", "B1", "A3", "A4", "B2", "C0", "Cr1", "Cl1", "Br3", "Bl3", "A5",
-    "A6", "B4", "Cr2", "Cl2", "A7", "D0", "D1", "C3", "F0", "B5", "Br6", "Bl6", "Cr4", "Cl4", "RA0",
-    "D2", "B7", "RA1", "D3", "Cr5", "Cl5", "F1", "D4", "C6", "Cr7", "Cl7", "RA2", "RY0", "RB1",
-    "RX1", "RA3", "D5", "D6", "D7", "RB0", "RX0", "F2", "RC1", "RY2", "RB3", "RX3", "F3", "RC0",
-    "RB2", "RX2", "RA4", "RA5", "GU0", "RC3", "RA6", "GD0", "RA7", "RC2", "GU1", "RB5", "RX5",
-    "GD1", "GU2", "RB6", "RX6", "GD2", "RY4", "RB7", "RX7", "GU3", "GD3", "RC5", "GU4", "GD4",
-    "GU5", "RB4", "RX4", "RC6", "GD5", "GU6", "GD6", "RC7", "GU7", "RC4", "GD7",
+    "A0", "A1", "Br0", "Bl0", "A2", "B1", "A3", "C0", "Br2", "Bl2", "Cr1", "Cl1", "A4", "B3", "C2",
+    "A5", "A7", "D0", "D1", "A6", "Cr3", "Cl3", "F0", "B4", "Br5", "Bl5", "D2", "RA0", "Br6", "Bl6",
+    "RA1", "B7", "D3", "Cr4", "Cl4", "F1", "RB0", "RX0", "RB1", "RX1", "C5", "C6", "RA2", "Cr7",
+    "Cl7", "RA3", "D4", "D5", "RC0", "D6", "RC1", "F2", "F3", "RA4", "RY3", "RA5", "RC2", "D7",
+    "RA6", "RB4", "RX4", "RB3", "RX3", "F4", "RB5", "RX5", "GU0", "GD0", "RC4", "RY6", "RA7", "RC3",
+    "GU1", "GD1", "GU2", "RC5", "RB6", "RX6", "GD2", "RB7", "RX7", "GU3", "GD3", "GU4", "GD4",
+    "RC6", "GU5", "GD5", "RC7", "GU6", "GD6", "GU7", "GD7",
 )
 
 root_half = 0.7071067811865476
@@ -87,8 +87,8 @@
     routes, gates, tok, grad, w_up, w_down,
     out, grad_up, grad_down,
     route_buf, gate_buf, values, sel, send_slots, xy, wu, wd, act, d_pre, part, from_mate, acc,
-    hop_a, hop_b, from_y, slots, result, final,
-    send_sem, recv_sem, own_sem,
+    hop_a, hop_b, hop_c, from_y, slots, result, final,
+    send_sem, recv_sem, own_sem, ready,
 ):
     z, y, c, x = place()
     k = ((y + 1) // 2) % 2
@@ -97,14 +97,11 @@
     mate = device(z, y, 1 - c, x)
     right, left, far = (x + 1) % X, (x + 3) % X, (x + 2) % X
     to_right, to_left = device(z, y, c, right), device(z, y, c, left)
-    to_y = device(z, partner, c, x)
+    to_y, to_far = device(z, partner, c, x), device(z, y, c, far)
 
     slots[...] = jnp.zeros_like(slots)
-    others = [mate, to_right, to_left]
-    for dz in NEAR[::-1]:
-        for row in (3 - partner, 3 - y, partner, y):
-            if dz or row is not y:
-                others.append(device((z + dz) % Z, row, c, x))
+    up, down = device((z + 1) % Z, y, c, x), device((z + Z - 1) % Z, y, c, x)
+    others = [mate, to_right, to_left, to_y, device(z, 3 - y, c, x), up, down]
     barrier = pltpu.get_barrier_semaphore()
     for other in others:
         pl.semaphore_signal(barrier, inc=1, device_id=other, device_id_type=MESH)
@@ -141,6 +138,16 @@
     total = jnp.dot(pick, mine, preferred_element_type=jnp.float32)
 
     pl.semaphore_wait(barrier, len(others))
+
+    def announce(r):
+        pl.semaphore_signal(ready.at[r, 0], inc=1, device_id=up, device_id_type=MESH)
+        pl.semaphore_signal(ready.at[r, 1], inc=1, device_id=down, device_id_type=MESH)
+
+    def hear(r):
+        pl.semaphore_wait(ready.at[r, 0], 1)
+        pl.semaphore_wait(ready.at[r, 1], 1)
+
+    announce(0)
     first = net.send(routes, route_buf, mate)
     second = net.send(gates, gate_buf, mate)
     third = net.make(tok, values, mate)
@@ -158,21 +165,34 @@
 
     first.wait_recv()
     second.wait_recv()
+    hear(0)
+    announce(1)
     pick, more = choose(route_buf[...], gate_buf[...], 1 - c)
     sel[1 - c] = pick
     scale = scale + more
+    hear(1)
+    announce(2)
     third.wait_recv()
     total = total + jnp.dot(pick, values[...], preferred_element_type=jnp.float32)
     total = total * jnp.where(c == 0, 1.0, scale)
     send_slots[...] = total.astype(jnp.bfloat16).reshape(EXPERTS, PAIR, QUARTER)
 
-    def cols(q, core=None):
-        if core is None:
-            return pl.ds(pl.multiple_of(q * QUARTER, QUARTER), QUARTER)
-        return pl.ds(pl.multiple_of(q * QUARTER + core * HALF, HALF), HALF)
+    def cols(q):
+        return pl.ds(pl.multiple_of(q * QUARTER, QUARTER), QUARTER)
 
     ev = {}
+    own_block = xy.at[c, k * 2 + y // 2, :, cols(x)]
+    own_slots = send_slots.at[z * 2 + y // 2]
+    ev["r", 0, "a"] = net.send(own_slots, own_block, to_right)
+    ev["l", 0, "a"] = net.send(own_slots, own_block, to_left)
+    ev["y", 0, "a"] = net.send(own_slots, own_block, to_y)
+    heard = 2
     for n, dz in enumerate(NEAR):
+        while heard < min(dz, Z - dz):
+            hear(heard)
+            heard += 1
+            if heard < 4:
+                announce(heard)
         ze = (z + dz) % Z
         for j in range(2):
             src = send_slots.at[ze * 2 + (y // 2 if j == 0 else 1 - y // 2)]
@@ -188,10 +208,11 @@
         ev[key] = net.send(ref, ref, target)
 
     def got(*keys):
-        for key in keys:
-            if key not in done:
-                done.add(key)
-                ev[key].wait_recv()
+        for name in keys:
+            for key in (name, name + ("a",)):
+                if key in ev and key not in done:
+                    done.add(key)
+                    ev[key].wait_recv()
 
     done = set()
 
@@ -201,10 +222,10 @@
         else:
             got(("z", n, 0))
         got(("z", n, 1))
-        own = n * 4 + k * 2
-        share(("r", n), own, 2, x, to_right)
-        share(("l", n), own, 2, x, to_left)
-        share(("y", n), own, 2, x, to_y)
+        own, count = (k * 2 + 1 - y // 2, 1) if n == 0 else (n * 4 + k * 2, 2)
+        share(("r", n), own, count, x, to_right)
+        share(("l", n), own, count, x, to_left)
+        share(("y", n), own, count, x, to_y)
 
     def step_B(n):
         got(("y", n))
@@ -263,12 +284,16 @@
         product = lax.dot_general(
             slope, wu[...], (((1,), (1,)), ((), ())), preferred_element_type=jnp.float32
         )
-        part[pl.ds(first_block, count)] = product.astype(jnp.bfloat16).reshape(count, PAIR, D)
+        for q in range(4):
+            for h in range(2):
+                at = q * QUARTER + h * HALF
+                part[h, q, pl.ds(first_block, count)] = (
+                    product[:, at : at + HALF].astype(jnp.bfloat16).reshape(count, PAIR, HALF)
+                )
         for n in GROUPS[g]:
-            for q in range(4):
-                ev["p", n, q] = net.send(
-                    part.at[pl.ds(n * 4, 4), :, cols(q, 1 - c)], from_mate.at[q, pl.ds(n * 4, 4)], mate
-                )
+            ev["p", n] = net.send(
+                part.at[1 - c, :, pl.ds(n * 4, 4)], from_mate.at[:, pl.ds(n * 4, 4)], mate
+            )
 
     def wide(value):
         return value.astype(jnp.float32)
@@ -277,12 +302,16 @@
         ref[...] = (wide(ref[...]) + wide(other[...])).astype(jnp.bfloat16)
 
     def step_RA(n):
+        got(("p", n))
         for q in range(4):
-            got(("p", n, q))
             acc[q, pl.ds(n * 4, 4)] = (
-                wide(part[pl.ds(n * 4, 4), :, cols(q, c)]) + wide(from_mate[q, pl.ds(n * 4, 4)])
+                wide(part[c, q, pl.ds(n * 4, 4)]) + wide(from_mate[q, pl.ds(n * 4, 4)])
             ).astype(jnp.bfloat16)
-        if RETURN_MODES[n]:
+        if RETURN_MODES[n] == 2:
+            ev["br", n] = net.send(acc.at[right, pl.ds(n * 4, 4)], hop_b.at[n, 0], to_right)
+            ev["bl", n] = net.send(acc.at[left, pl.ds(n * 4, 4)], hop_b.at[n, 1], to_left)
+            ev["far", n] = net.send(acc.at[far, pl.ds(n * 4, 4)], hop_c.at[n], to_far)
+        elif RETURN_MODES[n] == 1:
             ev["ry", n] = net.send(
                 acc.at[pl.ds(0, 4), pl.ds(n * 4 + (1 - k) * 2, 2)], from_y.at[n], to_y
             )
@@ -322,14 +351,19 @@
     def step_RC(n):
         got(("br", n), ("bl", n))
         own = n * 4 + k * 2
-        block, count = (own, 2) if RETURN_MODES[n] else (n * 4, 4)
+        single = RETURN_MODES[n] == 1
+        block, count = (own, 2) if single else (n * 4, 4)
         ref = acc.at[x, pl.ds(block, count)]
-        ref[...] = (
+        total = (
             wide(ref[...]) + wide(hop_b[n, 0, pl.ds(0, count)]) + wide(hop_b[n, 1, pl.ds(0, count)])
-        ).astype(jnp.bfloat16)
+        )
+        if RETURN_MODES[n] == 2:
+            got(("far", n))
+            total = total + wide(hop_c[n])
+        ref[...] = total.astype(jnp.bfloat16)
         zs = (z + Z - NEAR[n]) % Z
         other = n * 4 + (1 - k) * 2
-        for j in range(2 if RETURN_MODES[n] else 4):
+        for j in range(2 if single else 4):
             row = y if j % 2 == 0 else 3 - y
             block = own if j < 2 else other
             block = block + (y // 2 if j % 2 == 0 else 1 - y // 2)
@@ -432,11 +466,12 @@
             pltpu.VMEM((HID_DEV, D), bf16),
             pltpu.VMEM((ROWS, HID_DEV), bf16),
             pltpu.VMEM((ROWS, HID_DEV), bf16),
-            pltpu.VMEM((BLOCKS, PAIR, D), bf16),
+            pltpu.VMEM((2, 4, BLOCKS, PAIR, HALF), bf16),
             pltpu.VMEM((4, BLOCKS, PAIR, HALF), bf16),
             pltpu.VMEM((4, BLOCKS, PAIR, HALF), bf16),
             pltpu.VMEM((Z, 2, 2, PAIR, HALF), bf16),
             pltpu.VMEM((Z, 2, 4, PAIR, HALF), bf16),
+            pltpu.VMEM((Z, 4, PAIR, HALF), bf16),
             pltpu.VMEM((Z, 4, 2, PAIR, HALF), bf16),
             pltpu.VMEM((2, EXPERTS, PAIR, HALF), bf16),
             pltpu.VMEM((2, TOK, HALF), bf16),
@@ -444,6 +479,7 @@
             pltpu.SemaphoreType.DMA((224,)),
             pltpu.SemaphoreType.DMA((224,)),
             pltpu.SemaphoreType.DMA((4,)),
+            pltpu.SemaphoreType.REGULAR((4, 2)),
         ],
         compiler_params=pltpu.CompilerParams(
             collective_id=0, has_side_effects=True, vmem_limit_bytes=VMEM_MIB * 1024 * 1024

time: 95.2 us -> 93.5 us (0.982)
  Pallas kernels: 94.3 us -> 92.6 us
    pallas_call x1, Pallas kernels: 90.9 us -> 89.2 us  [local(): pl.pallas_call(kernel, out_shape=(pltpu.VMEM((TOK, QUARTER), bf16), pltpu...]
where the time goes in v4:
time: 93.5 us; the launch traced here: 93.4 us
  Pallas kernels  92.6 us (99%)
    pallas_call x1, Pallas kernels, local(): pl.pallas_call(kernel, out_shape=(pltpu.VMEM((TOK, QUARTER), bf16), pltpu...  89.2 us
    pallas_call x1, Pallas kernels, local(): pl.pallas_call(store_kernel, out_shape=tuple((jax.ShapeDtypeStruct(g.shap...  3.46 us

profile of v4, /device:TPU:1, one launch (start us, length us, event | category | flops | bytes accessed | tf_op | source)
XLA Modules:
  0.0 93.4 jit_solution(9704091938273133100)
XLA Ops:
  0.6 89.2 %expert_backward.1 = (bf16[128,512]{1,0:T(8,128)(2,1)S(1)}, f32[2048,512]{1,0:T(8,128)S(1)}, f32[512,2048]{1,0:T(8,128)S(1)}) custom-call(s32[2,128]{1,0:T(2,128)} %bitcast.2, f32[2,128]{1,0:T(2,128)} %bitcast.3, bf16[128,512]{1,0:T(8,128)(2,1)} %tok.1, bf16[128,512]{1,0:T(8,128)(2,1)} %grad.1, bf16[2048,512]{1,0:T(8,128)(2,1)} %w_up.1, bf16[512,2048]{1,0:T(8,128)(2,1)} %w_down.1), custom_call_target="tpu_custom_call" | custom-call | tf_op jit(solution)/shard_map/expert_backward/pallas_call | solution.py:449
  89.8 3.5 %store_grads.1 = (bf16[128,512]{1,0:T(8,128)(2,1)}, f32[2048,512]{1,0:T(8,128)}, f32[512,2048]{1,0:T(8,128)}) custom-call(bf16[128,512]{1,0:T(8,128)(2,1)S(1)} %get-tuple-element.6.tok, f32[2048,512]{1,0:T(8,128)S(1)} %get-tuple-element.7.up, f32[512,2048]{1,0:T(8,128)S(1)} %get-tuple-element.8.down), custom_call_target="tpu_custom_call" | custom-call | tf_op jit(solution)/shard_map/store_grads/pallas_call | solution.py:489

commit v5 on v4

--- a/solution.py
+++ b/solution.py
@@ -19,18 +19,18 @@
 TILE = 256
 PARTS = 1
 VMEM_MIB = 48
-NEAR = (0, 7, 2, 6, 4, 3, 5, 1)
-MODES = (1, 0, 1, 0, 0, 1, 1, 0)
-RETURN_MODES = (0, 0, 2, 1, 0, 0, 1, 0)
-GROUPS = ((0, 1), (2, 3), (4, 5), (6,), (7,))
+NEAR = (0, 1, 7, 4, 3, 5, 2, 6)
+MODES = (0, 1, 0, 1, 0, 0, 0, 1)
+RETURN_MODES = (1, 0, 1, 2, 0, 0, 0, 1)
+GROUPS = ((0, 1), (2, 3), (4, 5), (6, 7))
 ORDER = (
-    "A0", "A1", "Br0", "Bl0", "A2", "B1", "A3", "C0", "Br2", "Bl2", "Cr1", "Cl1", "A4", "B3", "C2",
-    "A5", "A7", "D0", "D1", "A6", "Cr3", "Cl3", "F0", "B4", "Br5", "Bl5", "D2", "RA0", "Br6", "Bl6",
-    "RA1", "B7", "D3", "Cr4", "Cl4", "F1", "RB0", "RX0", "RB1", "RX1", "C5", "C6", "RA2", "Cr7",
-    "Cl7", "RA3", "D4", "D5", "RC0", "D6", "RC1", "F2", "F3", "RA4", "RY3", "RA5", "RC2", "D7",
-    "RA6", "RB4", "RX4", "RB3", "RX3", "F4", "RB5", "RX5", "GU0", "GD0", "RC4", "RY6", "RA7", "RC3",
-    "GU1", "GD1", "GU2", "RC5", "RB6", "RX6", "GD2", "RB7", "RX7", "GU3", "GD3", "GU4", "GD4",
-    "RC6", "GU5", "GD5", "RC7", "GU6", "GD6", "GU7", "GD7",
+    "A0", "A1", "A2", "B0", "Br1", "Bl1", "A3", "B2", "Cr0", "Cl0", "C1", "Br3", "Bl3", "A4", "A5",
+    "Cr2", "Cl2", "D1", "A6", "A7", "D0", "C3", "F0", "B4", "D2", "B5", "RA0", "B6", "RA1", "Br7",
+    "Bl7", "Cr4", "Cl4", "D3", "Cr5", "Cl5", "F1", "RY0", "Cr6", "Cl6", "RB1", "RX1", "C7", "D4",
+    "RA2", "RA3", "D5", "D7", "RB0", "RX0", "D6", "F2", "RC1", "RY2", "F3", "RA4", "RA5", "GU0",
+    "RC0", "RC3", "RB2", "RX2", "GD0", "RA6", "RA7", "GU1", "GD1", "RB4", "RX4", "GU2", "RB5",
+    "RX5", "GD2", "RC2", "GU3", "RB6", "RX6", "GD3", "GU4", "RC4", "RY7", "RC5", "RB7", "RX7",
+    "RC6", "RC7", "GD4", "GU5", "GD5", "GU6", "GD6", "GU7", "GD7",
 )
 
 root_half = 0.7071067811865476
@@ -256,13 +256,16 @@
     def step_C(n):
         got(("fr", n), ("fl", n))
         share(("y3", n), n * 4 + k * 2, 2, far, to_y)
+        ref = xy.at[c, pl.ds(n * 4 + k * 2, 2)]
+        ev["m", n, "a"] = net.send(ref, ref, mate)
 
     def step_D(n):
         if MODES[n]:
             got(("y", n), ("y1", n), ("y2", n), ("y3", n))
+            ref = xy.at[c, pl.ds(n * 4 + (1 - k) * 2, 2)]
         else:
             got(("fr", n), ("fl", n))
-        ref = xy.at[c, pl.ds(n * 4, 4)]
+            ref = xy.at[c, pl.ds(n * 4, 4)]
         ev["m", n] = net.send(ref, ref, mate)
 
     def step_F(g):

time: 93.5 us -> 90 us (0.963)
  Pallas kernels: 92.6 us -> 89.1 us
    pallas_call x1, Pallas kernels: 89.2 us -> 85.6 us  [local(): pl.pallas_call(kernel, out_shape=(pltpu.VMEM((TOK, QUARTER), bf16), pltpu...]
where the time goes in v5:
time: 90 us; the launch traced here: 89.9 us
  Pallas kernels  89.1 us (99%)
    pallas_call x1, Pallas kernels, local(): pl.pallas_call(kernel, out_shape=(pltpu.VMEM((TOK, QUARTER), bf16), pltpu...  85.6 us
    pallas_call x1, Pallas kernels, local(): pl.pallas_call(store_kernel, out_shape=tuple((jax.ShapeDtypeStruct(g.shap...  3.46 us

profile of v5, /device:TPU:1, one launch (start us, length us, event | category | flops | bytes accessed | tf_op | source)
XLA Modules:
  0.0 89.9 jit_solution(2190462261753838024)
XLA Ops:
  0.6 85.6 %expert_backward.1 = (bf16[128,512]{1,0:T(8,128)(2,1)S(1)}, f32[2048,512]{1,0:T(8,128)S(1)}, f32[512,2048]{1,0:T(8,128)S(1)}) custom-call(s32[2,128]{1,0:T(2,128)} %bitcast.2, f32[2,128]{1,0:T(2,128)} %bitcast.3, bf16[128,512]{1,0:T(8,128)(2,1)} %tok.1, bf16[128,512]{1,0:T(8,128)(2,1)} %grad.1, bf16[2048,512]{1,0:T(8,128)(2,1)} %w_up.1, bf16[512,2048]{1,0:T(8,128)(2,1)} %w_down.1), custom_call_target="tpu_custom_call" | custom-call | tf_op jit(solution)/shard_map/expert_backward/pallas_call | solution.py:452
  86.3 3.5 %store_grads.1 = (bf16[128,512]{1,0:T(8,128)(2,1)}, f32[2048,512]{1,0:T(8,128)}, f32[512,2048]{1,0:T(8,128)}) custom-call(bf16[128,512]{1,0:T(8,128)(2,1)S(1)} %get-tuple-element.6.tok, f32[2048,512]{1,0:T(8,128)S(1)} %get-tuple-element.7.up, f32[512,2048]{1,0:T(8,128)S(1)} %get-tuple-element.8.down), custom_call_target="tpu_custom_call" | custom-call | tf_op jit(solution)/shard_map/store_grads/pallas_call | solution.py:492

commit v6 on v5

--- a/solution.py
+++ b/solution.py
@@ -306,21 +306,30 @@
 
     def step_RA(n):
         got(("p", n))
-        for q in range(4):
-            acc[q, pl.ds(n * 4, 4)] = (
-                wide(part[c, q, pl.ds(n * 4, 4)]) + wide(from_mate[q, pl.ds(n * 4, 4)])
-            ).astype(jnp.bfloat16)
+        blocks = pl.ds(n * 4, 4)
+
+        def both_cores(*quarters):
+            for q in quarters:
+                acc[q, blocks] = (wide(part[c, q, blocks]) + wide(from_mate[q, blocks])).astype(
+                    jnp.bfloat16
+                )
+
         if RETURN_MODES[n] == 2:
+            both_cores(far, right, left)
             ev["br", n] = net.send(acc.at[right, pl.ds(n * 4, 4)], hop_b.at[n, 0], to_right)
             ev["bl", n] = net.send(acc.at[left, pl.ds(n * 4, 4)], hop_b.at[n, 1], to_left)
             ev["far", n] = net.send(acc.at[far, pl.ds(n * 4, 4)], hop_c.at[n], to_far)
+            both_cores(x)
         elif RETURN_MODES[n] == 1:
+            both_cores(0, 1, 2, 3)
             ev["ry", n] = net.send(
                 acc.at[pl.ds(0, 4), pl.ds(n * 4 + (1 - k) * 2, 2)], from_y.at[n], to_y
             )
         else:
+            both_cores(far)
             ev["ar", n] = net.send(acc.at[far, pl.ds(n * 4, 2)], hop_a.at[n, 0], to_right)
             ev["al", n] = net.send(acc.at[far, pl.ds(n * 4 + 2, 2)], hop_a.at[n, 1], to_left)
+            both_cores(right, left, x)
 
     def step_RY(n):
         got(("ry", n))

time: 90 us -> 90 us (level)
  no operation moved by 1% of the time
where the time goes in v6:
time: 90 us; the launch traced here: 89.9 us
  Pallas kernels  89.1 us (99%)
    pallas_call x1, Pallas kernels, local(): pl.pallas_call(kernel, out_shape=(pltpu.VMEM((TOK, QUARTER), bf16), pltpu...  85.6 us
    pallas_call x1, Pallas kernels, local(): pl.pallas_call(store_kernel, out_shape=tuple((jax.ShapeDtypeStruct(g.shap...  3.46 us

profile of v6, /device:TPU:1, one launch (start us, length us, event | category | flops | bytes accessed | tf_op | source)
XLA Modules:
  0.0 89.9 jit_solution(2150587500578894035)
XLA Ops:
  0.6 85.6 %expert_backward.1 = (bf16[128,512]{1,0:T(8,128)(2,1)S(1)}, f32[2048,512]{1,0:T(8,128)S(1)}, f32[512,2048]{1,0:T(8,128)S(1)}) custom-call(s32[2,128]{1,0:T(2,128)} %bitcast.2, f32[2,128]{1,0:T(2,128)} %bitcast.3, bf16[128,512]{1,0:T(8,128)(2,1)} %tok.1, bf16[128,512]{1,0:T(8,128)(2,1)} %grad.1, bf16[2048,512]{1,0:T(8,128)(2,1)} %w_up.1, bf16[512,2048]{1,0:T(8,128)(2,1)} %w_down.1), custom_call_target="tpu_custom_call" | custom-call | tf_op jit(solution)/shard_map/expert_backward/pallas_call | solution.py:461
  86.3 3.5 %store_grads.1 = (bf16[128,512]{1,0:T(8,128)(2,1)}, f32[2048,512]{1,0:T(8,128)}, f32[512,2048]{1,0:T(8,128)}) custom-call(bf16[128,512]{1,0:T(8,128)(2,1)S(1)} %get-tuple-element.6.tok, f32[2048,512]{1,0:T(8,128)S(1)} %get-tuple-element.7.up, f32[512,2048]{1,0:T(8,128)S(1)} %get-tuple-element.8.down), custom_call_target="tpu_custom_call" | custom-call | tf_op jit(solution)/shard_map/store_grads/pallas_call | solution.py:501
